TPU v7x, 256 devices: a whole 4x4x8 slice. The times are simulated.
256 devices in a mesh: wa: 16 (over y_hi, z), dev: 16 (over y_lo, x, core).
Axes of the slice: x: 4, y: 4 (y_hi: 2, y_lo: 2; y = y_hi * 2 + y_lo), z: 8, core: 2. Of those that a mesh axis runs over, the one named last changes fastest.
Arguments:
- output_gradient: bfloat16 [2048, 8192], P('wa'), may hold values from -6 to 6
- down_weight: bfloat16 [28672, 8192], P('dev', 'wa'), may hold values from -0.03125 to 0.03125
- gate_preactivation: bfloat16 [2048, 28672], P('wa', 'dev'), may hold values from -6 to 6
- up_preactivation: bfloat16 [2048, 28672], P('wa', 'dev'), may hold values from -6 to 6
- adapter_down_factor: bfloat16 [16, 16, 28672], P(None, None, 'dev'), may hold values from -0.0625 to 0.0625
- adapter_up_factor: bfloat16 [16, 16, 8192], P(None, None, 'dev'), may hold values from -0.0625 to 0.0625
- tile_owner_adapter: int32 [128, 1], replicated, may hold values from 0 to 15
- tile_live_count: int32 [128], replicated, may hold values from 1 to 16
Outputs:
- grad_gate: bfloat16 [2048, 28672], P('wa', 'dev')
- grad_up: bfloat16 [2048, 28672], P('wa', 'dev')
- grad_a: float32 [16, 16, 28672], P('wa', None, 'dev')
- grad_b: float32 [16, 16, 8192], P('wa', None, 'dev')
Inputs may be any that keep to these rules, and one draw needn't show every extreme that they name: `tile_owner_adapter`: every one of the 16 adapters owns at least one tile.
All inputs are finite; a program needn't handle non-finite values.
Results may differ from a plain program's by a relative error of at most 0.013.
Values may be sent and summed in bfloat16 or wider, within the bound.
A program may use at most 128 MiB of HBM per device.

v0:
```python
import jax
import jax.numpy as jnp
from jax import lax
from jax.sharding import PartitionSpec as P

TILE = 16


def on_device(
    output_gradient,
    down_weight,
    gate_preactivation,
    up_preactivation,
    adapter_down_factor,
    adapter_up_factor,
    tile_owner_adapter,
    tile_live_count,
):
    wa_index = lax.axis_index("wa")
    dev_index = lax.axis_index("dev")
    token_rows = output_gradient.shape[0]
    hidden_local = down_weight.shape[0]
    wa_cols = down_weight.shape[1]
    shard_columns = adapter_up_factor.shape[2]
    adapter_list = adapter_down_factor.shape[0]
    adapter_rank_rows = adapter_down_factor.shape[1]
    tiles_local = token_rows // TILE
    own_adapter = lax.dynamic_slice_in_dim(
        tile_owner_adapter[:, 0], wa_index * tiles_local, tiles_local
    )
    own_live = lax.dynamic_slice_in_dim(tile_live_count, wa_index * tiles_local, tiles_local)
    row_adapter = jnp.repeat(own_adapter, TILE)
    position = jnp.arange(token_rows) % TILE
    live_rows = position < jnp.repeat(own_live, TILE)
    masked_rows = jnp.where(
        live_rows[:, None], output_gradient, jnp.zeros((), output_gradient.dtype)
    )
    gate_wide = gate_preactivation.astype(jnp.float32)
    up_wide = up_preactivation.astype(jnp.float32)
    hidden_state = (jax.nn.silu(gate_wide) * up_wide).astype(jnp.bfloat16)
    shard_piece = lax.all_gather(down_weight, "wa", axis=1, tiled=True)
    groups = shard_piece.shape[1] // wa_cols
    left = masked_rows.reshape(token_rows, groups, wa_cols)
    right = shard_piece.reshape(hidden_local, groups, wa_cols)
    partial_value = jnp.einsum("tkc,fkc->ktf", left, right, preferred_element_type=jnp.float32)
    rounded = lax.optimization_barrier(partial_value.astype(jnp.bfloat16))
    base_grad = jnp.sum(rounded.astype(jnp.float32), axis=0)
    selector = row_adapter[:, None] == jnp.arange(adapter_list, dtype=jnp.int32)[None, :]
    flattened_down = adapter_down_factor.reshape(adapter_list * adapter_rank_rows, hidden_local)
    flattened_up = adapter_up_factor.reshape(adapter_list * adapter_rank_rows, shard_columns)

    def choose_rows(complete_value):
        reshaped_value = complete_value.reshape(token_rows, adapter_list, adapter_rank_rows)
        return jnp.sum(
            jnp.where(selector[:, :, None], reshaped_value, jnp.zeros((), complete_value.dtype)),
            axis=1,
        )

    def spread_value(values):
        wide_value = jnp.where(
            selector[:, :, None], values[:, None, :], jnp.zeros((), values.dtype)
        )
        return wide_value.reshape(token_rows, adapter_list * adapter_rank_rows)

    grad_slice = lax.dynamic_slice_in_dim(masked_rows, dev_index * shard_columns, shard_columns, 1)
    in_partial = choose_rows(
        lax.dot_general(
            hidden_state,
            flattened_down,
            (((1,), (1,)), ((), ())),
            preferred_element_type=jnp.float32,
        )
    )
    out_partial = choose_rows(
        lax.dot_general(
            grad_slice, flattened_up, (((1,), (1,)), ((), ())), preferred_element_type=jnp.float32
        )
    )
    in_summed, out_summed = lax.psum((in_partial, out_partial), "dev")
    spread_input = spread_value(in_summed.astype(jnp.bfloat16))
    spread_output = spread_value(out_summed.astype(jnp.bfloat16))
    hidden_grad = base_grad + 2.0 * jnp.dot(
        spread_output, flattened_down, preferred_element_type=jnp.float32
    )
    sigmoid_gate = jax.nn.sigmoid(gate_wide)
    grad_up = (hidden_grad * gate_wide * sigmoid_gate).astype(jnp.bfloat16)
    grad_gate = (
        hidden_grad * up_wide * sigmoid_gate * (1.0 + gate_wide * (1.0 - sigmoid_gate))
    ).astype(jnp.bfloat16)
    down_factor_partial = 2.0 * lax.dot_general(
        spread_output, hidden_state, (((0,), (0,)), ((), ())), preferred_element_type=jnp.float32
    )
    up_factor_partial = 2.0 * lax.dot_general(
        spread_input, grad_slice, (((0,), (0,)), ((), ())), preferred_element_type=jnp.float32
    )
    down_factor_partial = down_factor_partial.reshape(adapter_list, adapter_rank_rows, hidden_local)
    up_factor_partial = up_factor_partial.reshape(adapter_list, adapter_rank_rows, shard_columns)
    grad_a, grad_b = (
        lax.psum_scatter(down_factor_partial, "wa", scatter_dimension=0, tiled=True),
        lax.psum_scatter(up_factor_partial, "wa", scatter_dimension=0, tiled=True),
    )
    return (grad_gate, grad_up, grad_a, grad_b)


def solution(mesh):
    placed = (
        P("wa", None),
        P("dev", "wa"),
        P("wa", "dev"),
        P("wa", "dev"),
        P(None, None, "dev"),
        P(None, None, "dev"),
        P(),
        P(),
    )
    return jax.shard_map(
        on_device,
        mesh=mesh,
        in_specs=placed,
        out_specs=(P("wa", "dev"), P("wa", "dev"), P("wa", None, "dev"), P("wa", None, "dev")),
        check_vma=False,
    )
```

profile of v0, /device:TPU:2, one launch (start us, length us, event | category | flops | bytes accessed | tf_op | source)
XLA Modules:
  0.0 798.2 jit_solution(14165972701911176698)
XLA Ops:
  7.2 0.0 copy-start
  7.2 0.0 copy-start.5
  7.2 0.0 all-gather.2.cloned.1.call-start
  7.2 3.9 copy.13
  11.2 0.0 all-gather.2.cloned.1.call-update
  11.2 0.0 reduce-scatter.5.cloned.1.call-start
  11.2 0.0 copy-done.5
  11.3 0.1 dynamic_slice.11
  11.3 0.1 broadcast_in_dim.69
  11.4 0.1 reshape.82
  11.5 0.0 copy-done.6
  11.5 0.1 dynamic-slice_bitcast_fusion
  11.6 0.1 broadcast_in_dim.72
  11.6 0.1 eq.21
  11.7 0.0 copy-start.1
  11.8 0.0 copy-start.2
  11.8 0.0 copy-start.3
  11.8 1.9 broadcast_select_fusion
  13.7 0.2 fusion.5
  14.0 0.5 fusion.4
  14.5 52.8 %all-reduce = (bf16[128,16]{0,1:T(8,128)(2,1)S(1)}, bf16[128,16]{0,1:T(8,128)(2,1)S(1)}) all-reduce(f32[128,16]{0,1:T(8,128)S(1)} %fusion.5, f32[128,16]{0,1:T(8,128)S(1)} %fusion.4), channel_id=1, replica_groups=mesh['wa'=16,'dev'=16] {'dev'}, use_global_device_ids=true, to_apply=%region_2.3 | all-reduce | flops 4096 | bytes 24576 | tf_op jit(solution)/shard_map/psum | solution.py:79
  67.3 1.0 convolution_multiply_fusion.1
  68.3 0.0 reduce-scatter.5.cloned.1.call-update
  68.4 0.0 reduce-scatter.3.cloned.1.call-start
  68.4 2.9 convolution_multiply_fusion
  71.3 0.0 reduce-scatter.3.cloned.1.call-update
  71.3 308.6 %all-gather.2.cloned.1.call-done = bf16[1792,8192]{0,1:T(8,128)(2,1)} async-done(((bf16[1792,512]{0,1:T(8,128)(2,1)}), bf16[1792,8192]{0,1:T(8,128)(2,1)}) %all-gather.2.cloned.1.call-update) | async-done | bytes 29360144 | tf_op jit(solution)/shard_map/all_gather | solution.py:41
  379.9 16.4 %convolution_convert_fusion = bf16[16,128,1792]{2,1,0:T(8,128)(2,1)} fusion(bf16[1792,16,512]{0,2,1:T(8,128)(2,1)} %bitcast.29, bf16[16,16,8,512]{3,2,1,0:T(8,128)(2,1)S(1)} %bitcast.30), kind=kOutput, calls=%fused_computation.1 | convolution fusion | flops 3761766400 | bytes 38797312 | tf_op jit(solution)/shard_map/tkc,fkc->ktf/dot_general | solution.py:45
  396.3 4.3 convert_reduce_fusion
  400.6 1.6 fusion.15
  402.2 178.1 %reduce-scatter.5.cloned.1.call-done = f32[1,16,512]{2,1,0:T(8,128)} async-done(((f32[16,16,512]{2,1,0:T(8,128)}), f32[1,16,512]{2,1,0:T(8,128)}) %reduce-scatter.5.cloned.1.call-update) | async-done | bytes 32784 | tf_op jit(solution)/shard_map/reduce_scatter | solution.py:100
  580.3 211.3 %reduce-scatter.3.cloned.1.call-done = f32[1,16,1792]{2,1,0:T(8,128)} async-done(((f32[16,16,1792]{2,1,0:T(8,128)}), f32[1,16,1792]{2,1,0:T(8,128)}) %reduce-scatter.3.cloned.1.call-update) | async-done | bytes 114704 | tf_op jit(solution)/shard_map/reduce_scatter | solution.py:99
  (10 shorter events, 0.0 us)
Async XLA Ops:
  7.2 6.8 copy-start
  7.2 4.1 copy-start.5
  7.2 4.3 copy-start.6
  7.2 372.7 %all-gather.2.cloned.1.call-start = ((), (), s32[]{:S(2)}) async-start(), calls=%async_computation.2 | async-start | bytes 31195136 | tf_op jit(solution)/shard_map/all_gather | solution.py:41
  11.2 569.1 %reduce-scatter.5.cloned.1.call-start = ((), (), s32[]{:S(2)}) async-start(), calls=%async_computation.4 | async-start | bytes 557056 | tf_op jit(solution)/shard_map/reduce_scatter | solution.py:100
  11.7 1.9 copy-start.1
  11.8 2.2 copy-start.2
  11.8 2.2 copy-start.3
  68.4 723.3 %reduce-scatter.3.cloned.1.call-start = ((), (), s32[]{:S(2)}) async-start(), calls=%async_computation.3 | async-start | bytes 1949696 | tf_op jit(solution)/shard_map/reduce_scatter | solution.py:99
  396.3 4.3 copy-start.4
Sparse Core Ops, SparseCore 0:
  11.3 368.5 all-gather.1
  384.2 196.0 reduce-scatter.4
  584.8 206.8 reduce-scatter.2
where the time goes:
time: 798 us
  waiting for transfers between devices  698 us (87%)
  blocking collectives  52.8 us (7%)
  matrix products  22.7 us (3%)
  between operations  13.9 us (2%)
    all_gather x1, waiting for transfers between devices, on_device(): shard_piece = lax.all_gather(down_weight, 'wa', axis=1, tiled=True)  309 us
    reduce_scatter x1, waiting for transfers between devices, on_device(): lax.psum_scatter(down_factor_partial, 'wa', scatter_dimension=0, tiled=True)  211 us
    reduce_scatter x1, waiting for transfers between devices, on_device(): lax.psum_scatter(up_factor_partial, 'wa', scatter_dimension=0, tiled=True)  178 us
    psum x1, blocking collectives, on_device(): in_summed, out_summed = lax.psum((in_partial, out_partial), 'dev')  52.8 us
    dot_general x1, matrix products, on_device(): jnp.einsum('tkc,fkc->ktf', left, right, preferred_element_type=jnp.float32)  16.4 us
  transfers between devices with their start and end apart: 3, of which 3 were waited for; matrix products, arithmetic and copies ran while one was open for 4% of the time, Pallas kernels for 0%

commit v1 on v0

v1 whole, which is shorter than its diff:
```python
import jax
import jax.numpy as jnp
from jax import lax
from jax.experimental import pallas as pl
from jax.experimental.pallas import tpu as pltpu
from jax.sharding import PartitionSpec as P

TILE = 16
NZ, NY, NX, NC = 8, 4, 4, 2
NDEV = 16
ROWS = 128
KG = 512
HID = 1792
CH = 128
NCH = HID // CH
NPAIR = NCH // 2
RANK = 16
ADAPTERS = 16
AR = RANK * ADAPTERS
MESH = pl.DeviceIdType.MESH
NT = (((1,), (1,)), ((), ()))
F32 = jnp.float32
BF16 = jnp.bfloat16
OFFSETS = (0, 1, 7, 2, 6, 3, 5, 4)


def sigmoid(v):
    return 1.0 / (1.0 + jnp.exp(-v))


def kernel(
    g_ref, w_ref, gate_ref, up_ref, a_ref, b_ref, owner_ref, live_ref,
    ogate_ref, oup_ref, oga_ref, ogb_ref,
    gs, gf, wu, wd, w2, hid, part, rbuf, sbuf, pg, rg, sg, tg, tb, gr, gsl, lo, lb, sel,
    w1_s, w1_r, wr_s, wr_r, z_s, z_r, x_s, x_r, xr_s, xr_r, c_s, c_r, l_s, l_r,
    b_s, b_r, a_s, a_r, y_s, y_r,
):
    wa = lax.axis_index("wa")
    dev = lax.axis_index("dev")
    yh, z = lax.div(wa, NZ), lax.rem(wa, NZ)
    yl, low = lax.div(dev, 8), lax.rem(dev, 8)
    x, c = lax.div(low, 2), lax.rem(low, 2)
    sh = c * 4 + x
    y = yh * 2 + yl

    def y_device(step):
        other = lax.rem(y + step, NY)
        return (lax.div(other, 2) * NZ + z, lax.rem(other, 2) * 8 + low)

    up_dev, down_dev, far_dev = y_device(1), y_device(3), y_device(2)

    def z_device(off):
        return (yh * NZ + lax.rem(z + off, NZ), dev)

    def x_index(step):
        return lax.rem(x + step, NX)

    def x_device(step):
        return (wa, yl * 8 + x_index(step) * 2 + c)

    core_dev = (wa, yl * 8 + x * 2 + (1 - c))

    def dev_device(off):
        return (wa, lax.rem(dev + off, NDEV))

    def copy(src, dst, ssem, rsem, target):
        return pltpu.make_async_remote_copy(
            src_ref=src, dst_ref=dst, send_sem=ssem, recv_sem=rsem,
            device_id=target, device_id_type=MESH,
        )

    barrier = pltpu.get_barrier_semaphore()
    peers = [z_device(o) for o in range(1, NZ)] + [dev_device(o) for o in range(1, NDEV)]
    peers += [up_dev, down_dev, far_dev]
    for peer in peers:
        pl.semaphore_signal(barrier, inc=1, device_id=peer, device_id_type=MESH)

    live = live_ref[...].astype(F32)
    tile_lane = lax.broadcasted_iota(jnp.int32, (1, 128), 1)
    share_live = jnp.sum(
        jnp.where(tile_lane == wa * 8 + sh, live, 0.0), axis=1, keepdims=True
    )
    row16 = lax.broadcasted_iota(jnp.int32, (TILE, KG), 0).astype(F32)
    keep16 = row16 < share_live
    for q in range(NZ):
        for h in range(2):
            group = (yh if h == 0 else 1 - yh) * NZ + q
            cols = pl.ds(pl.multiple_of(group * KG, KG), KG)
            rows = pl.ds(pl.multiple_of(sh * TILE, TILE), TILE)
            piece = jnp.where(keep16, g_ref[rows, cols], jnp.zeros((), BF16))
            gs[q, :, h * KG : (h + 1) * KG] = piece
    gf[pl.ds(z, 1), pl.ds(sh, 1)] = gs[pl.ds(z, 1)].reshape(1, 1, TILE, 2 * KG)

    def w_first(j):
        copy(w_ref.at[pl.ds(pl.multiple_of(2 * j * CH, CH), CH)], wu.at[j],
             w1_s.at[0, j], w1_r.at[0, j], up_dev).start()
        copy(w_ref.at[pl.ds(pl.multiple_of((2 * j + 1) * CH, CH), CH)], wd.at[j],
             w1_s.at[1, j], w1_r.at[1, j], down_dev).start()

    def w_relay(j):
        r0 = copy(wu.at[j], w2.at[2 * j], wr_s.at[0, j], wr_r.at[0, j], up_dev)
        r1 = copy(wd.at[j], w2.at[2 * j + 1], wr_s.at[1, j], wr_r.at[1, j], down_dev)
        return r0, r1

    def w_step(j):
        for d, buf, target in ((0, wu, up_dev), (1, wd, down_dev)):
            copy(buf.at[j], buf.at[j], w1_s.at[d, j], w1_r.at[d, j], target).wait_recv()
        r0, r1 = w_relay(j)
        r0.start()
        r1.start()

    def z_send(off):
        zt = lax.rem(z + off, NZ)
        return copy(gs.at[zt], gf.at[z, sh], z_s.at[off], z_r.at[off], z_device(off))

    def source(q):
        return lax.rem(z + OFFSETS[q], NZ)

    def share_of(step):
        return c * 4 + x_index(step)

    def x_send(q, d):
        band = gf.at[source(q), sh]
        return copy(band, band, x_s.at[d, q], x_r.at[d, q], x_device(1 if d == 0 else 3))

    def x_recv(q, d):
        band = gf.at[source(q), share_of(3 if d == 0 else 1)]
        return copy(band, band, x_s.at[d, q], x_r.at[d, q], x_device(1 if d == 0 else 3))

    def x_relay(q):
        if q % 2 == 0:
            band, target = gf.at[source(q), share_of(3)], x_device(1)
        else:
            band, target = gf.at[source(q), share_of(1)], x_device(3)
        return copy(band, band, xr_s.at[q], xr_r.at[q], target)

    def x_relay_recv(q):
        band = gf.at[source(q), share_of(2)]
        return copy(band, band, xr_s.at[q], xr_r.at[q], x_device(1))

    def core_send(q):
        block = gf.at[source(q), pl.ds(c * 4, 4)]
        return copy(block, block, c_s.at[q], c_r.at[q], core_dev)

    def core_recv(q):
        block = gf.at[source(q), pl.ds((1 - c) * 4, 4)]
        return copy(block, block, c_s.at[q], c_r.at[q], core_dev)

    def stage_a(q):
        if q > 0:
            off = NZ - OFFSETS[q]
            band = gf.at[source(q), sh]
            copy(band, band, z_s.at[off], z_r.at[off], z_device(off)).wait_recv()
        x_send(q, 0).start()
        x_send(q, 1).start()

    def stage_b(q):
        x_recv(q, 0).wait_recv()
        x_recv(q, 1).wait_recv()
        x_relay(q).start()

    def stage_c(q):
        x_relay_recv(q).wait_recv()
        core_send(q).start()

    def g_tick(t):
        if t < NZ:
            stage_a(t)
        if 0 <= t - 1 < NZ:
            stage_b(t - 1)
        if 0 <= t - 2 < NZ:
            stage_c(t - 2)
        if 0 <= t - 3 < NZ:
            core_recv(t - 3).wait_recv()

    pl.semaphore_wait(barrier, len(peers))
    for off in (4, 3, 5, 2, 6, 1, 7):
        z_send(off).start()
    for j in range(3):
        w_first(j)
    g_tick(0)

    def hidden_step(k, acc):
        cols = pl.ds(pl.multiple_of(k * 256, 256), 256)
        gate = gate_ref[:, cols].astype(F32)
        value = (gate * sigmoid(gate) * up_ref[:, cols].astype(F32)).astype(BF16)
        hid[:, cols] = value
        return acc + lax.dot_general(a_ref[:, cols], value, NT, preferred_element_type=F32)

    in_full = lax.fori_loop(0, HID // 256, hidden_step, jnp.zeros((AR, ROWS), F32))
    lane_tile = lax.broadcasted_iota(jnp.int32, (ROWS, 128), 1)
    sub_row = lax.broadcasted_iota(jnp.int32, (ROWS, 128), 0)
    pick = lane_tile == wa * 8 + lax.shift_right_logical(sub_row, 4)
    row_live = jnp.sum(jnp.where(pick, live, 0.0), axis=1, keepdims=True)
    position = lax.rem(lax.broadcasted_iota(jnp.int32, (ROWS, KG), 0), TILE).astype(F32)
    own_cols = pl.ds(pl.multiple_of(dev * KG, KG), KG)
    sliced = jnp.where(position < row_live, g_ref[:, own_cols], jnp.zeros((), BF16))
    gsl[...] = sliced
    out_full = lax.dot_general(b_ref[...], sliced, NT, preferred_element_type=F32)
    pick_t = sub_row == wa * 8 + lax.shift_right_logical(lane_tile, 4)
    owner_lane = jnp.sum(
        jnp.where(pick_t, owner_ref[...].astype(F32), 0.0), axis=0, keepdims=True
    )
    adapter_row = lax.shift_right_logical(
        lax.broadcasted_iota(jnp.int32, (AR, ROWS), 0), 4
    ).astype(F32)
    selected = jnp.where(adapter_row == owner_lane, 1.0, 0.0)
    sel[...] = selected

    def choose(full):
        kept = jnp.where(selected > 0.5, full, 0.0)
        return jnp.sum(kept.reshape(ADAPTERS, RANK, ROWS), axis=0)

    lb[0, 0:RANK] = choose(in_full)
    lb[0, RANK : 2 * RANK] = choose(out_full)

    def l_copy(off):
        return copy(lb.at[0], lb.at[off], l_s.at[off], l_r.at[off], dev_device(off))

    for off in range(1, NDEV):
        l_copy(off).start()

    for t in range(1, 5):
        g_tick(t)
    w_step(0)
    w_first(3)
    for t in range(5, 8):
        g_tick(t)

    for off in range(1, NDEV):
        l_copy(off).wait_recv()
    total = jnp.zeros((2 * RANK, ROWS), F32)
    for src in range(NDEV):
        total = total + lb[lax.rem(dev + NDEV - src, NDEV)]
    summed = total.astype(BF16).astype(F32)
    keep = sel[...] > 0.5

    def spread(values):
        wide = jnp.broadcast_to(values[None], (ADAPTERS, RANK, ROWS)).reshape(AR, ROWS)
        return jnp.where(keep, wide, 0.0)

    spread_in = spread(summed[0:RANK]).astype(BF16)
    spread_out_wide = spread(summed[RANK : 2 * RANK])
    spread_out = spread_out_wide.astype(BF16)
    spread_out_t = spread_out_wide.T.astype(BF16)

    def adapter_step(k, carry):
        cols = pl.ds(pl.multiple_of(k * 256, 256), 256)
        grad = 2.0 * jnp.dot(spread_out, hid[:, cols], preferred_element_type=F32)
        pg[:, :, cols] = grad.reshape(ADAPTERS, RANK, 256)
        lo[:, cols] = 2.0 * jnp.dot(spread_out_t, a_ref[:, cols], preferred_element_type=F32)
        return carry

    lax.fori_loop(0, HID // 256, adapter_step, 0)
    grad_b = 2.0 * jnp.dot(spread_in, gsl[...], preferred_element_type=F32)
    pg[:, :, HID : HID + KG] = grad_b.reshape(ADAPTERS, RANK, KG)

    w_step(1)
    w_first(4)
    for t in range(8, NZ + 3):
        g_tick(t)

    def z_next(d):
        return (yh * NZ + lax.rem(z + 1 + 6 * d, NZ), dev)

    def target_z(d, s):
        return lax.rem(z + NZ + (4 - s) * (1 - 2 * d), NZ)

    def b_copy(src, d, ch, s):
        return copy(src, rbuf.at[d, ch, s], b_s.at[d, ch, s], b_r.at[d, ch, s], z_next(d))

    def a_copy(src, d, k, s):
        return copy(src, rg.at[d, k, s], a_s.at[d, k, s], a_r.at[d, k, s], z_next(d))

    def base_first(ch, d, s):
        sbuf[ch, s] = part[ch, target_z(d, s)].astype(BF16)
        b_copy(sbuf.at[ch, s], d, ch, s).start()

    def base_forward(ch, d, s):
        slot = rbuf.at[d, ch, s - 1]
        b_copy(slot, d, ch, s - 1).wait_recv()
        slot[...] = (slot[...].astype(F32) + part[ch, target_z(d, s)]).astype(BF16)
        b_copy(slot, d, ch, s).start()

    def base_last(ch):
        for d in range(2):
            b_copy(rbuf.at[d, ch, 3], d, ch, 3).wait_recv()
        cols = pl.ds(pl.multiple_of(ch * CH, CH), CH)
        base = part[ch, z] + rbuf[0, ch, 3].astype(F32) + rbuf[1, ch, 3].astype(F32)
        grad = base + lo[:, cols]
        gate = gate_ref[:, cols].astype(F32)
        up_value = up_ref[:, cols].astype(F32)
        s = sigmoid(gate)
        oup_ref[:, cols] = (grad * gate * s).astype(BF16)
        ogate_ref[:, cols] = (grad * up_value * s * (1.0 + gate * (1.0 - s))).astype(BF16)

    def adapter_first(k, d, s):
        sg[k, s] = pg[k * NZ + target_z(d, s)].astype(BF16)
        a_copy(sg.at[k, s], d, k, s).start()

    def adapter_forward(k, d, s):
        slot = rg.at[d, k, s - 1]
        a_copy(slot, d, k, s - 1).wait_recv()
        slot[...] = (slot[...].astype(F32) + pg[k * NZ + target_z(d, s)]).astype(BF16)
        a_copy(slot, d, k, s).start()

    def adapter_last(k):
        for d in range(2):
            a_copy(rg.at[d, k, 3], d, k, 3).wait_recv()
        done = pg[k * NZ + z] + rg[0, k, 3].astype(F32) + rg[1, k, 3].astype(F32)
        tg[k] = done
        tb[k] = done.astype(BF16)

    def adapter_out():
        return copy(tb.at[1 - yh], gr, y_s, y_r, far_dev)

    def product(j):
        for d, target in ((0, up_dev), (1, down_dev)):
            got = w2.at[2 * j + d]
            copy(got, got, wr_s.at[d, j], wr_r.at[d, j], target).wait_recv()
        rows = pl.ds(pl.multiple_of(j * 2 * CH, CH), 2 * CH)
        mine = w_ref[rows, :]
        other = w2[pl.ds(2 * j, 2)].reshape(2 * CH, KG)

        def block(k, carry):
            left = gf[pl.ds(2 * k, 2)].reshape(2 * ROWS, 2 * KG)
            value = lax.dot_general(left[:, :KG], mine, NT, preferred_element_type=F32)
            value = value + lax.dot_general(left[:, KG:], other, NT, preferred_element_type=F32)
            value = value.reshape(2, ROWS, 2 * CH)
            part[2 * j, pl.ds(2 * k, 2)] = value[:, :, :CH]
            part[2 * j + 1, pl.ds(2 * k, 2)] = value[:, :, CH:]
            return carry

        lax.fori_loop(0, NZ // 2, block, 0)

    def tick(t, carry):
        for k in range(2):
            for s in (1, 2, 3):
                @pl.when(t == k + s)
                def _(k=k, s=s):
                    d4 = k % 2
                    adapter_forward(k, d4, s)
                    if s == 1:
                        adapter_first(k, 1 - d4, s)
                    else:
                        adapter_forward(k, 1 - d4, s)

            @pl.when(t == k)
            def _(k=k):
                adapter_first(k, k % 2, 0)

        for s in (3, 2, 1):
            ch = t - s

            @pl.when((ch >= 0) & (ch < NCH))
            def _(ch=ch, s=s):
                d4 = lax.rem(ch, 2)
                base_forward(ch, d4, s)
                if s == 1:
                    base_first(ch, 1 - d4, s)
                else:
                    base_forward(ch, 1 - d4, s)

        @pl.when((t < NCH) & (lax.rem(t, 2) == 0))
        def _():
            product(lax.div(t, 2))

        @pl.when(t < NCH)
        def _():
            base_first(t, lax.rem(t, 2), 0)

        ch = t - 4

        @pl.when(ch >= 0)
        def _():
            base_last(ch)

        @pl.when((lax.rem(t, 2) == 1) & (t < 10))
        def _():
            j = lax.div(t - 1, 2) + 2
            w_step(j)

            @pl.when(j + 3 < NPAIR)
            def _():
                w_first(j + 3)

        for k in range(2):
            @pl.when(t == k + 4)
            def _(k=k):
                adapter_last(k)

        @pl.when(t == 6)
        def _():
            adapter_out().start()

        return carry

    lax.fori_loop(0, NCH + 4, tick, 0)

    adapter_out().wait_recv()
    final = tg[yh] + gr[...].astype(F32)
    oga_ref[...] = final[:, :HID]
    ogb_ref[...] = final[:, HID:]

    adapter_out().wait_send()
    for off in range(1, NZ):
        z_send(off).wait_send()
    for off in range(1, NDEV):
        l_copy(off).wait_send()
    for q in range(NZ):
        x_send(q, 0).wait_send()
        x_send(q, 1).wait_send()
        x_relay(q).wait_send()
        core_send(q).wait_send()
    for k in range(2):
        for d in range(2):
            for s in range(4):
                if s > 0 or d == k % 2:
                    a_copy(rg.at[d, k, s], d, k, s).wait_send()

    def drain_w(j, carry):
        for d, buf, target in ((0, wu, up_dev), (1, wd, down_dev)):
            copy(buf.at[j], buf.at[j], w1_s.at[d, j], w1_r.at[d, j], target).wait_send()
        r0, r1 = w_relay(j)
        r0.wait_send()
        r1.wait_send()
        return carry

    lax.fori_loop(0, NPAIR, drain_w, 0)

    def drain_b(ch, carry):
        d4 = lax.rem(ch, 2)
        b_copy(rbuf.at[d4, ch, 0], d4, ch, 0).wait_send()
        for d in range(2):
            for s in range(1, 4):
                b_copy(rbuf.at[d, ch, s], d, ch, s).wait_send()
        return carry

    lax.fori_loop(0, NCH, drain_b, 0)


def on_device(grad, weight, gate, up, down_factor, up_factor, owner, live):
    dma = pltpu.SemaphoreType.DMA
    vmem = pltpu.VMEM
    whole = pl.BlockSpec(memory_space=pltpu.VMEM)
    outs = pl.pallas_call(
        kernel,
        out_shape=(
            jax.ShapeDtypeStruct((ROWS, HID), BF16),
            jax.ShapeDtypeStruct((ROWS, HID), BF16),
            jax.ShapeDtypeStruct((RANK, HID), F32),
            jax.ShapeDtypeStruct((RANK, KG), F32),
        ),
        in_specs=[whole] * 8,
        out_specs=(whole,) * 4,
        scratch_shapes=[
            vmem((NZ, TILE, 2 * KG), BF16),
            vmem((NZ, 8, TILE, 2 * KG), BF16),
            vmem((NPAIR, CH, KG), BF16),
            vmem((NPAIR, CH, KG), BF16),
            vmem((NCH, CH, KG), BF16),
            vmem((ROWS, HID), BF16),
            vmem((NCH, NZ, ROWS, CH), F32),
            vmem((2, NCH, 4, ROWS, CH), BF16),
            vmem((NCH, 2, ROWS, CH), BF16),
            vmem((ADAPTERS, RANK, HID + KG), F32),
            vmem((2, 2, 4, RANK, HID + KG), BF16),
            vmem((2, 2, RANK, HID + KG), BF16),
            vmem((2, RANK, HID + KG), F32),
            vmem((2, RANK, HID + KG), BF16),
            vmem((RANK, HID + KG), BF16),
            vmem((ROWS, KG), BF16),
            vmem((ROWS, HID), F32),
            vmem((NDEV, 2 * RANK, ROWS), F32),
            vmem((AR, ROWS), F32),
            dma((2, NPAIR)), dma((2, NPAIR)),
            dma((2, NPAIR)), dma((2, NPAIR)),
            dma((NZ,)), dma((NZ,)),
            dma((2, NZ)), dma((2, NZ)),
            dma((NZ,)), dma((NZ,)),
            dma((NZ,)), dma((NZ,)),
            dma((NDEV,)), dma((NDEV,)),
            dma((2, NCH, 4)), dma((2, NCH, 4)),
            dma((2, 2, 4)), dma((2, 2, 4)),
            dma, dma,
        ],
        compiler_params=pltpu.CompilerParams(
            collective_id=0, has_side_effects=True, vmem_limit_bytes=60 * 1024 * 1024
        ),
    )(
        grad, weight, gate, up,
        down_factor.reshape(AR, HID), up_factor.reshape(AR, KG),
        owner, live.reshape(1, live.shape[0]),
    )
    out_gate, out_up, grad_a, grad_b = outs
    return out_gate, out_up, grad_a[None], grad_b[None]


def solution(mesh):
    placed = (
        P("wa", None),
        P("dev", "wa"),
        P("wa", "dev"),
        P("wa", "dev"),
        P(None, None, "dev"),
        P(None, None, "dev"),
        P(),
        P(),
    )
    return jax.shard_map(
        on_device,
        mesh=mesh,
        in_specs=placed,
        out_specs=(P("wa", "dev"), P("wa", "dev"), P("wa", None, "dev"), P("wa", None, "dev")),
        check_vma=False,
    )
```

time: 798 us -> 131 us (0.16)
  waiting for transfers between devices: 698 us -> 0 us
  Pallas kernels: 0 us -> 120 us
  blocking collectives: 52.8 us -> 0 us
  matrix products: 22.7 us -> 0 us
  between operations: 13.9 us -> 0.65 us
    reduce_scatter x2 -> x0, waiting for transfers between devices: 389 us -> none  [the longest x1 211 us: on_device(): lax.psum_scatter(down_factor_partial, 'wa', scatter_dimension=0, tiled=True)]
    all_gather x1 -> x0, waiting for transfers between devices: 309 us -> none  [on_device(): shard_piece = lax.all_gather(down_weight, 'wa', axis=1, tiled=True)]
    pallas_call x0 -> x1, Pallas kernels: none -> 120 us  [on_device(): pl.pallas_call(kernel, out_shape=(jax.ShapeDtypeStruct((ROWS, HID), BF16)...]
    psum x1 -> x0, blocking collectives: 52.8 us -> none  [on_device(): in_summed, out_summed = lax.psum((in_partial, out_partial), 'dev')]
    dot_general x6 -> x0, matrix products: 22.7 us -> none  [the longest x1 16.4 us: on_device(): jnp.einsum('tkc,fkc->ktf', left, right, preferred_element_type=jnp.float32)]
  transfers between devices with their start and end apart: 3 -> 0, of which waited for: 3 -> 0; matrix products, arithmetic and copies ran while one was open for 4% -> 0% of each run, Pallas kernels for 0% -> 0%
where the time goes in v1:
time: 131 us; the launch traced here: 128 us
  Pallas kernels  120 us (92%)
  local copies, waits for them, and re-layouts  7.19 us (5%)
    pallas_call x1, Pallas kernels, on_device(): pl.pallas_call(kernel, out_shape=(jax.ShapeDtypeStruct((ROWS, HID), BF16)...  120 us
    unnamed x7, local copies, waits for them, and re-layouts  7.19 us

profile of v1, /device:TPU:2, one launch (start us, length us, event | category | flops | bytes accessed | tf_op | source)
XLA Modules:
  0.0 127.9 jit_solution(5679524287858312536)
XLA Ops:
  0.6 1.4 %copy.12.owner_ref = s32[128,1]{1,0:T(8,128)} copy(s32[128,1]{0,1:T(1,128)} %param.14) | data formatting | bytes 1024 | tf_op args[6]
  2.0 120.1 %shard_map.111 = (bf16[128,1792]{1,0:T(8,128)(2,1)}, bf16[128,1792]{1,0:T(8,128)(2,1)}, f32[16,1792]{1,0:T(8,128)}, f32[16,512]{1,0:T(8,128)}) custom-call(bf16[128,8192]{1,0:T(8,128)(2,1)} %g_ref.1, bf16[1792,512]{1,0:T(8,128)(2,1)} %w_ref.1, bf16[128,1792]{1,0:T(8,128)(2,1)} %gate_ref.1, bf16[128,1792]{1,0:T(8,128)(2,1)} %up_ref.1, ...), custom_call_target="tpu_custom_call" | custom-call | tf_op jit(solution)/shard_map/pallas_call | solution.py:446
  122.1 0.0 copy-start
  122.1 1.8 %copy.17 = bf16[128,1792]{1,0:T(8,128)(2,1)} copy(bf16[128,1792]{1,0:T(8,128)(2,1)} %get-tuple-element.16) | data formatting | bytes 917504
  123.9 1.8 %copy.18 = bf16[128,1792]{1,0:T(8,128)(2,1)} copy(bf16[128,1792]{1,0:T(8,128)(2,1)} %get-tuple-element.17) | data formatting | bytes 917504
  125.8 1.6 %copy.19 = f32[1,16,1792]{2,1,0:T(8,128)} copy(f32[1,16,1792]{2,1,0:T(8,128)} %bitcast.7) | data formatting | bytes 229376
  127.3 0.0 copy-done
  127.3 0.6 copy.20
Async XLA Ops:
  122.1 5.2 %copy-start = (f32[16,512]{1,0:T(8,128)S(1)}, f32[16,512]{1,0:T(8,128)}, u32[]{:S(2)}) copy-start(f32[16,512]{1,0:T(8,128)} %get-tuple-element.11) | copy-start | bytes 98308

commit v2 on v1

v2 whole, which is shorter than its diff:
```python
import jax
import jax.numpy as jnp
from jax import lax
from jax.experimental import pallas as pl
from jax.experimental.pallas import tpu as pltpu
from jax.sharding import PartitionSpec as P

TILE = 16
NZ, NY, NX, NC = 8, 4, 4, 2
NDEV = 16
ROWS = 128
KG = 512
HID = 1792
CH = 128
NCH = HID // CH
NPAIR = NCH // 2
LAG = 2
GCOL = HID + 512
GHALF = GCOL // 2
GTICK = 6
EARLY_W = 4
RANK = 16
ADAPTERS = 16
AR = RANK * ADAPTERS
MESH = pl.DeviceIdType.MESH
NT = (((1,), (1,)), ((), ()))
F32 = jnp.float32
BF16 = jnp.bfloat16
OFFSETS = (0, 1, 7, 2, 6, 3, 5, 4)


def sigmoid(v):
    return 1.0 / (1.0 + jnp.exp(-v))


def kernel(
    g_any, w_any, gate_any, up_any, a_any, b_any, owner_ref, live_ref,
    hg_ref, og_ref,
    w_ref, a_ref, b_ref, gate_ref, up_ref, gsh,
    gs, gf, w2, hid, part, rbuf, sbuf, pg, rg, sg, sgf, grf, gsl, lo, lb, sel,
    ld, w_s, w_r, z_s, z_r, x_s, x_r, c_s, c_r, l_s, l_r,
    b_s, b_r, a_s, a_r, y_s, y_r,
):
    wa = lax.axis_index("wa")
    dev = lax.axis_index("dev")
    yh, z = lax.div(wa, NZ), lax.rem(wa, NZ)
    yl, low = lax.div(dev, 8), lax.rem(dev, 8)
    x, c = lax.div(low, 2), lax.rem(low, 2)
    sh = c * 4 + x

    far_dev = ((1 - yh) * NZ + z, dev)

    def z_device(off):
        return (yh * NZ + lax.rem(z + off, NZ), dev)

    def x_index(step):
        return lax.rem(x + step, NX)

    def x_device(step):
        return (wa, yl * 8 + x_index(step) * 2 + c)

    core_dev = (wa, yl * 8 + x * 2 + (1 - c))

    def dev_device(off):
        return (wa, lax.rem(dev + off, NDEV))

    def copy(src, dst, ssem, rsem, target):
        return pltpu.make_async_remote_copy(
            src_ref=src, dst_ref=dst, send_sem=ssem, recv_sem=rsem,
            device_id=target, device_id_type=MESH,
        )

    barrier = pltpu.get_barrier_semaphore()
    peers = [z_device(o) for o in (4, 3, 5, 2, 6, 1, 7)] + [far_dev]
    peers += [dev_device(o) for o in range(1, NDEV)]
    for peer in peers:
        pl.semaphore_signal(barrier, inc=1, device_id=peer, device_id_type=MESH)

    own_cols = pl.ds(pl.multiple_of(dev * KG, KG), KG)
    share_rows = pl.ds(pl.multiple_of(sh * TILE, TILE), TILE)
    loads = [
        pltpu.make_async_copy(src, dst, ld.at[i])
        for i, (src, dst) in enumerate(
            (
                (g_any.at[share_rows], gsh),
                (gate_any, gate_ref),
                (up_any, up_ref),
                (a_any, a_ref),
                (g_any.at[:, own_cols], gsl),
                (b_any, b_ref),
                (w_any, w_ref),
            )
        )
    ]
    for load in loads:
        load.start()

    live = live_ref[...].astype(F32)
    tile_lane = lax.broadcasted_iota(jnp.int32, (1, 128), 1)
    share_live = jnp.sum(
        jnp.where(tile_lane == wa * 8 + sh, live, 0.0), axis=1, keepdims=True
    )
    row16 = lax.broadcasted_iota(jnp.int32, (TILE, KG), 0).astype(F32)
    keep16 = row16 < share_live
    loads[0].wait()
    for q in range(NZ):
        for h in range(2):
            group = (yh if h == 0 else 1 - yh) * NZ + q
            cols = pl.ds(pl.multiple_of(group * KG, KG), KG)
            piece = jnp.where(keep16, gsh[:, cols], jnp.zeros((), BF16))
            gs[q, :, h * KG : (h + 1) * KG] = piece
    gf[pl.ds(z, 1), pl.ds(sh, 1)] = gs[pl.ds(z, 1)].reshape(1, 1, TILE, 2 * KG)

    def hidden_step(k, acc):
        cols = pl.ds(pl.multiple_of(k * 256, 256), 256)
        gate = gate_ref[:, cols].astype(F32)
        value = (gate * sigmoid(gate) * up_ref[:, cols].astype(F32)).astype(BF16)
        hid[:, cols] = value
        return acc + lax.dot_general(a_ref[:, cols], value, NT, preferred_element_type=F32)

    for i in (1, 2, 3):
        loads[i].wait()
    in_full = lax.fori_loop(0, HID // 256, hidden_step, jnp.zeros((AR, ROWS), F32))
    lane_tile = lax.broadcasted_iota(jnp.int32, (ROWS, 128), 1)
    sub_row = lax.broadcasted_iota(jnp.int32, (ROWS, 128), 0)
    pick = lane_tile == wa * 8 + lax.shift_right_logical(sub_row, 4)
    row_live = jnp.sum(jnp.where(pick, live, 0.0), axis=1, keepdims=True)
    position = lax.rem(lax.broadcasted_iota(jnp.int32, (ROWS, KG), 0), TILE).astype(F32)
    loads[4].wait()
    sliced = jnp.where(position < row_live, gsl[...], jnp.zeros((), BF16))
    gsl[...] = sliced
    loads[5].wait()
    out_full = lax.dot_general(b_ref[...], sliced, NT, preferred_element_type=F32)
    pick_t = sub_row == wa * 8 + lax.shift_right_logical(lane_tile, 4)
    owners = jnp.broadcast_to(owner_ref[...].astype(F32), (8, 128)).astype(BF16)
    chosen = jnp.where(pick_t, 1.0, 0.0).astype(BF16)
    owner_lane = jnp.dot(owners, chosen, preferred_element_type=F32)[0:1]
    adapter_row = lax.shift_right_logical(
        lax.broadcasted_iota(jnp.int32, (AR, ROWS), 0), 4
    ).astype(F32)
    selected = jnp.where(adapter_row == owner_lane, 1.0, 0.0)
    sel[...] = selected

    def choose(full):
        kept = jnp.where(selected > 0.5, full, 0.0)
        return jnp.sum(kept.reshape(ADAPTERS, RANK, ROWS), axis=0)

    lb[0, 0:RANK] = choose(in_full)
    lb[0, RANK : 2 * RANK] = choose(out_full)

    def l_copy(off):
        return copy(lb.at[0], lb.at[off], l_s.at[off], l_r.at[off], dev_device(off))

    def w_copy(j):
        rows = pl.ds(pl.multiple_of(j * 2 * CH, 2 * CH), 2 * CH)
        return copy(w_any.at[rows], w2.at[rows], w_s.at[j], w_r.at[j], far_dev)

    def z_send(off):
        zt = lax.rem(z + off, NZ)
        return copy(gs.at[zt], gf.at[z, sh], z_s.at[off], z_r.at[off], z_device(off))

    def source(q):
        return lax.rem(z + OFFSETS[q], NZ)

    def x_send(q, step):
        band = gf.at[source(q), sh]
        return copy(band, band, x_s.at[step, q], x_r.at[step, q], x_device(step))

    def x_recv(q, step):
        band = gf.at[source(q), c * 4 + x_index(NX - step)]
        return copy(band, band, x_s.at[step, q], x_r.at[step, q], x_device(step))

    def core_send(q):
        block = gf.at[source(q), pl.ds(c * 4, 4)]
        return copy(block, block, c_s.at[q], c_r.at[q], core_dev)

    def core_recv(q):
        block = gf.at[source(q), pl.ds((1 - c) * 4, 4)]
        return copy(block, block, c_s.at[q], c_r.at[q], core_dev)

    pl.semaphore_wait(barrier, len(peers))
    for off in (1, 7, 2, 6, 3, 5, 4):
        z_send(off).start()
    for j in range(EARLY_W):
        w_copy(j).start()
    for off in range(1, NDEV):
        l_copy(off).start()
    for q in range(NZ):
        if q > 0:
            off = NZ - OFFSETS[q]
            band = gf.at[source(q), sh]
            copy(band, band, z_s.at[off], z_r.at[off], z_device(off)).wait_recv()
        for step in (1, 3, 2):
            x_send(q, step).start()

    for off in range(1, NDEV):
        l_copy(off).wait_recv()
    total = jnp.zeros((2 * RANK, ROWS), F32)
    for src in range(NDEV):
        total = total + lb[lax.rem(dev + NDEV - src, NDEV)]
    summed = total.astype(BF16).astype(F32)
    keep = sel[...] > 0.5

    def spread(values):
        wide = jnp.broadcast_to(values[None], (ADAPTERS, RANK, ROWS)).reshape(AR, ROWS)
        return jnp.where(keep, wide, 0.0)

    spread_in = spread(summed[0:RANK]).astype(BF16)
    spread_out_wide = spread(summed[RANK : 2 * RANK])
    spread_out = spread_out_wide.astype(BF16)
    spread_out_t = spread_out_wide.T.astype(BF16)

    def adapter_step(k, carry):
        cols = pl.ds(pl.multiple_of(k * 256, 256), 256)
        grad = 2.0 * jnp.dot(spread_out, hid[:, cols], preferred_element_type=F32)
        pg[:, :, cols] = grad.reshape(ADAPTERS, RANK, 256)
        lo[:, cols] = 2.0 * jnp.dot(spread_out_t, a_ref[:, cols], preferred_element_type=F32)
        return carry

    lax.fori_loop(0, HID // 256, adapter_step, 0)
    grad_b = 2.0 * jnp.dot(spread_in, gsl[...], preferred_element_type=F32)
    pg[:, :, HID : HID + KG] = grad_b.reshape(ADAPTERS, RANK, KG)
    for q in range(NZ):
        sgf[q] = pg[(1 - yh) * NZ + q].astype(BF16)

    def adapter_exchange():
        return copy(sgf, grf, y_s, y_r, far_dev)

    adapter_exchange().start()
    for j in range(EARLY_W, NPAIR):
        w_copy(j).start()

    for q in range(NZ):
        for step in (1, 3, 2):
            x_recv(q, step).wait_recv()
        core_send(q).start()
    for q in range(NZ):
        core_recv(q).wait_recv()
    loads[6].wait()

    def z_next(d):
        return (yh * NZ + lax.rem(z + 1 + 6 * d, NZ), dev)

    def target_z(d, s):
        return lax.rem(z + NZ + (4 - s) * (1 - 2 * d), NZ)

    def b_copy(src, d, ch, s):
        return copy(src, rbuf.at[d, ch, s], b_s.at[d, ch, s], b_r.at[d, ch, s], z_next(d))

    def a_copy(src, d, k, s):
        return copy(src, rg.at[d, k, s], a_s.at[d, k, s], a_r.at[d, k, s], z_next(d))

    def base_first(ch, d, s):
        sbuf[ch, s] = part[ch, target_z(d, s)].astype(BF16)
        b_copy(sbuf.at[ch, s], d, ch, s).start()

    def base_forward(ch, d, s):
        slot = rbuf.at[d, ch, s - 1]
        b_copy(slot, d, ch, s - 1).wait_recv()
        slot[...] = (slot[...].astype(F32) + part[ch, target_z(d, s)]).astype(BF16)
        b_copy(slot, d, ch, s).start()

    def base_last(ch):
        for d in range(2):
            b_copy(rbuf.at[d, ch, 3], d, ch, 3).wait_recv()
        cols = pl.ds(pl.multiple_of(ch * CH, CH), CH)
        base = part[ch, z] + rbuf[0, ch, 3].astype(F32) + rbuf[1, ch, 3].astype(F32)
        hg_ref[:, cols] = base + lo[:, cols]

    def own_grads(k, zt):
        cols = slice(k * GHALF, (k + 1) * GHALF)
        return pg[yh * NZ + zt, :, cols] + grf[zt, :, cols].astype(F32)

    def adapter_first(k, d, s):
        sg[k, s] = own_grads(k, target_z(d, s)).astype(BF16)
        a_copy(sg.at[k, s], d, k, s).start()

    def adapter_forward(k, d, s):
        slot = rg.at[d, k, s - 1]
        a_copy(slot, d, k, s - 1).wait_recv()
        slot[...] = (slot[...].astype(F32) + own_grads(k, target_z(d, s))).astype(BF16)
        a_copy(slot, d, k, s).start()

    def adapter_last(k):
        for d in range(2):
            a_copy(rg.at[d, k, 3], d, k, 3).wait_recv()
        og_ref[:, k * GHALF : (k + 1) * GHALF] = (
            own_grads(k, z) + rg[0, k, 3].astype(F32) + rg[1, k, 3].astype(F32)
        )

    def product(j):
        rows = pl.ds(pl.multiple_of(j * 2 * CH, 2 * CH), 2 * CH)
        w_copy(j).wait_recv()
        mine = w_ref[rows, :]
        other = w2[rows, :]

        def block(k, carry):
            left = gf[pl.ds(2 * k, 2)].reshape(2 * ROWS, 2 * KG)
            value = lax.dot_general(left[:, :KG], mine, NT, preferred_element_type=F32)
            value = value + lax.dot_general(left[:, KG:], other, NT, preferred_element_type=F32)
            value = value.reshape(2, ROWS, 2 * CH)
            part[2 * j, pl.ds(2 * k, 2)] = value[:, :, :CH]
            part[2 * j + 1, pl.ds(2 * k, 2)] = value[:, :, CH:]
            return carry

        lax.fori_loop(0, NZ // 2, block, 0)

    def tick(t, carry):
        @pl.when((t < NCH) & (lax.rem(t, 2) == 0))
        def _():
            product(lax.div(t, 2))

        @pl.when(t < NCH)
        def _():
            base_first(t, lax.rem(t, 2), 0)

        for s in (1, 2, 3):
            ch = t - s * LAG

            @pl.when((ch >= 0) & (ch < NCH))
            def _(ch=ch, s=s):
                d4 = lax.rem(ch, 2)
                base_forward(ch, d4, s)
                if s == 1:
                    base_first(ch, 1 - d4, s)
                else:
                    base_forward(ch, 1 - d4, s)

        @pl.when(t == GTICK)
        def _():
            adapter_exchange().wait_recv()

        for k in range(2):
            @pl.when(t == GTICK + k)
            def _(k=k):
                adapter_first(k, k % 2, 0)

            for s in (1, 2, 3):
                @pl.when(t == GTICK + k + s * LAG)
                def _(k=k, s=s):
                    d4 = k % 2
                    adapter_forward(k, d4, s)
                    if s == 1:
                        adapter_first(k, 1 - d4, s)
                    else:
                        adapter_forward(k, 1 - d4, s)

            @pl.when(t == GTICK + k + 4 * LAG)
            def _(k=k):
                adapter_last(k)

        ch = t - 4 * LAG

        @pl.when(ch >= 0)
        def _():
            base_last(ch)

        return carry

    lax.fori_loop(0, NCH + 4 * LAG, tick, 0)

    adapter_exchange().wait_send()
    for off in range(1, NZ):
        z_send(off).wait_send()
    for off in range(1, NDEV):
        l_copy(off).wait_send()
    for q in range(NZ):
        for step in (1, 2, 3):
            x_send(q, step).wait_send()
        core_send(q).wait_send()
    for j in range(NPAIR):
        w_copy(j).wait_send()
    for k in range(2):
        for d in range(2):
            for s in range(4):
                if s > 0 or d == k % 2:
                    a_copy(rg.at[d, k, s], d, k, s).wait_send()

    def drain_b(ch, carry):
        d4 = lax.rem(ch, 2)
        b_copy(rbuf.at[d4, ch, 0], d4, ch, 0).wait_send()
        for d in range(2):
            for s in range(1, 4):
                b_copy(rbuf.at[d, ch, s], d, ch, s).wait_send()
        return carry

    lax.fori_loop(0, NCH, drain_b, 0)


def finish(hg_ref, og_ref, gate_ref, up_ref, ogate_ref, oup_ref, oga_ref, ogb_ref):
    oga_ref[...] = og_ref[:, :HID]
    ogb_ref[...] = og_ref[:, HID:]

    def step(k, carry):
        cols = pl.ds(pl.multiple_of(k * 256, 256), 256)
        grad = hg_ref[:, cols]
        gate = gate_ref[:, cols].astype(F32)
        up_value = up_ref[:, cols].astype(F32)
        s = sigmoid(gate)
        oup_ref[:, cols] = (grad * gate * s).astype(BF16)
        ogate_ref[:, cols] = (grad * up_value * s * (1.0 + gate * (1.0 - s))).astype(BF16)
        return carry

    lax.fori_loop(0, HID // 256, step, 0)


def on_device(grad, weight, gate, up, down_factor, up_factor, owner, live):
    dma = pltpu.SemaphoreType.DMA
    vmem = pltpu.VMEM
    whole = pl.BlockSpec(memory_space=pltpu.VMEM)
    anywhere = pl.BlockSpec(memory_space=pl.ANY)
    hidden_grad, adapter_grads = pl.pallas_call(
        kernel,
        out_shape=(
            jax.ShapeDtypeStruct((ROWS, HID), F32),
            jax.ShapeDtypeStruct((RANK, GCOL), F32),
        ),
        in_specs=[anywhere] * 6 + [whole] * 2,
        out_specs=(whole,) * 2,
        scratch_shapes=[
            vmem((HID, KG), BF16),
            vmem((AR, HID), BF16),
            vmem((AR, KG), BF16),
            vmem((ROWS, HID), BF16),
            vmem((ROWS, HID), BF16),
            vmem((TILE, 16 * KG), BF16),
            vmem((NZ, TILE, 2 * KG), BF16),
            vmem((NZ, 8, TILE, 2 * KG), BF16),
            vmem((HID, KG), BF16),
            vmem((ROWS, HID), BF16),
            vmem((NCH, NZ, ROWS, CH), F32),
            vmem((2, NCH, 4, ROWS, CH), BF16),
            vmem((NCH, 2, ROWS, CH), BF16),
            vmem((ADAPTERS, RANK, GCOL), F32),
            vmem((2, 2, 4, RANK, GHALF), BF16),
            vmem((2, 2, RANK, GHALF), BF16),
            vmem((NZ, RANK, GCOL), BF16),
            vmem((NZ, RANK, GCOL), BF16),
            vmem((ROWS, KG), BF16),
            vmem((ROWS, HID), F32),
            vmem((NDEV, 2 * RANK, ROWS), F32),
            vmem((AR, ROWS), F32),
            dma((7,)),
            dma((NPAIR,)), dma((NPAIR,)),
            dma((NZ,)), dma((NZ,)),
            dma((NX, NZ)), dma((NX, NZ)),
            dma((NZ,)), dma((NZ,)),
            dma((NDEV,)), dma((NDEV,)),
            dma((2, NCH, 4)), dma((2, NCH, 4)),
            dma((2, 2, 4)), dma((2, 2, 4)),
            dma, dma,
        ],
        compiler_params=pltpu.CompilerParams(
            collective_id=0, has_side_effects=True, vmem_limit_bytes=60 * 1024 * 1024
        ),
    )(
        grad, weight, gate, up,
        down_factor.reshape(AR, HID), up_factor.reshape(AR, KG),
        owner.reshape(1, owner.shape[0]), live.reshape(1, live.shape[0]),
    )
    out_gate, out_up, grad_a, grad_b = pl.pallas_call(
        finish,
        out_shape=(
            jax.ShapeDtypeStruct((ROWS, HID), BF16),
            jax.ShapeDtypeStruct((ROWS, HID), BF16),
            jax.ShapeDtypeStruct((RANK, HID), F32),
            jax.ShapeDtypeStruct((RANK, KG), F32),
        ),
        in_specs=[whole] * 4,
        out_specs=(whole,) * 4,
    )(hidden_grad, adapter_grads, gate, up)
    return out_gate, out_up, grad_a[None], grad_b[None]


def solution(mesh):
    placed = (
        P("wa", None),
        P("dev", "wa"),
        P("wa", "dev"),
        P("wa", "dev"),
        P(None, None, "dev"),
        P(None, None, "dev"),
        P(),
        P(),
    )
    return jax.shard_map(
        on_device,
        mesh=mesh,
        in_specs=placed,
        out_specs=(P("wa", "dev"), P("wa", "dev"), P("wa", None, "dev"), P("wa", None, "dev")),
        check_vma=False,
    )
```

time: 131 us -> 102 us (0.78); the launches traced: 128 us -> 102 us
  Pallas kernels: 120 us -> 101 us
  local copies, waits for them, and re-layouts: 7.19 us -> 0 us
    pallas_call x1 -> x2, Pallas kernels: 120 us -> 101 us  [the longest x1 98.1 us: on_device(): pl.pallas_call(kernel, out_shape=(jax.ShapeDtypeStruct((ROWS, HID), F32),...]
    unnamed x7 -> x0, local copies, waits for them, and re-layouts: 7.19 us -> none
where the time goes in v2:
time: 102 us
  Pallas kernels  101 us (99%)
    pallas_call x1, Pallas kernels, on_device(): pl.pallas_call(kernel, out_shape=(jax.ShapeDtypeStruct((ROWS, HID), F32),...  98.1 us
    pallas_call x1, Pallas kernels, on_device(): pl.pallas_call(finish, out_shape=(jax.ShapeDtypeStruct((ROWS, HID), BF16)...  2.99 us

profile of v2, /device:TPU:2, one launch (start us, length us, event | category | flops | bytes accessed | tf_op | source)
XLA Modules:
  0.0 101.7 jit_solution(15386809160893833933)
XLA Ops:
  0.6 98.1 %shard_map.111 = (f32[128,1792]{1,0:T(8,128)}, f32[16,2304]{1,0:T(8,128)}) custom-call(bf16[128,8192]{1,0:T(8,128)(2,1)} %g_any.1, bf16[1792,512]{1,0:T(8,128)(2,1)} %w_any.1, bf16[128,1792]{1,0:T(8,128)(2,1)} %gate_ref.1, bf16[128,1792]{1,0:T(8,128)(2,1)} %up_ref.1, bf16[256,1792]{1,0:T(8,128)(2,1)} %bitcast.6, bf16[256,512]{1,0:T(8,128)(2,1)} %bitcast.7, ...), custom_call_target="tpu_custom_call" | custom-call | tf_op jit(solution)/shard_map/pallas_call | solution.py:412
  98.7 3.0 %shard_map.112 = (bf16[128,1792]{1,0:T(8,128)(2,1)}, bf16[128,1792]{1,0:T(8,128)(2,1)}, f32[16,1792]{1,0:T(8,128)}, f32[16,512]{1,0:T(8,128)}) custom-call(f32[128,1792]{1,0:T(8,128)} %get-tuple-element.10.hg_ref, f32[16,2304]{1,0:T(8,128)} %get-tuple-element.11.og_ref, bf16[128,1792]{1,0:T(8,128)(2,1)} %gate_ref.1, bf16[128,1792]{1,0:T(8,128)(2,1)} %up_ref.1), custom_call_target="tpu_custom_call" | custom-call | tf_op jit(solution)/shard_map/pallas_call | solution.py:461

commit v3 on v2

--- a/solution.py
+++ b/solution.py
@@ -17,8 +17,11 @@
 LAG = 2
 GCOL = HID + 512
 GHALF = GCOL // 2
-GTICK = 6
-EARLY_W = 4
+GTICK = 8
+ATICK = 5
+EARLY_W = 2
+FH = HID // 2
+GH = KG // 2
 RANK = 16
 ADAPTERS = 16
 AR = RANK * ADAPTERS
@@ -37,9 +40,9 @@
     g_any, w_any, gate_any, up_any, a_any, b_any, owner_ref, live_ref,
     hg_ref, og_ref,
     w_ref, a_ref, b_ref, gate_ref, up_ref, gsh,
-    gs, gf, w2, hid, part, rbuf, sbuf, pg, rg, sg, sgf, grf, gsl, lo, lb, sel,
+    gs, gf, w2, hid, part, rbuf, sbuf, pg, rg, sg, hs, hx, so, lx, tg, tb, gr, gsl, lo, lb, sel,
     ld, w_s, w_r, z_s, z_r, x_s, x_r, c_s, c_r, l_s, l_r,
-    b_s, b_r, a_s, a_r, y_s, y_r,
+    b_s, b_r, a_s, a_r, h_s, h_r, k_s, k_r, y_s, y_r,
 ):
     wa = lax.axis_index("wa")
     dev = lax.axis_index("dev")
@@ -131,15 +134,25 @@
     gsl[...] = sliced
     loads[5].wait()
     out_full = lax.dot_general(b_ref[...], sliced, NT, preferred_element_type=F32)
-    pick_t = sub_row == wa * 8 + lax.shift_right_logical(lane_tile, 4)
+    far_half = 1 - yh
+    hs[:, :FH] = hid[:, pl.ds(pl.multiple_of(far_half * FH, 128), FH)]
+    hs[:, FH:] = gsl[:, pl.ds(pl.multiple_of(far_half * GH, 128), GH)]
+    hx[0, :, :FH] = hid[:, pl.ds(pl.multiple_of(yh * FH, 128), FH)]
+    hx[0, :, FH:] = gsl[:, pl.ds(pl.multiple_of(yh * GH, 128), GH)]
     owners = jnp.broadcast_to(owner_ref[...].astype(F32), (8, 128)).astype(BF16)
-    chosen = jnp.where(pick_t, 1.0, 0.0).astype(BF16)
-    owner_lane = jnp.dot(owners, chosen, preferred_element_type=F32)[0:1]
     adapter_row = lax.shift_right_logical(
         lax.broadcasted_iota(jnp.int32, (AR, ROWS), 0), 4
     ).astype(F32)
-    selected = jnp.where(adapter_row == owner_lane, 1.0, 0.0)
-    sel[...] = selected
+
+    def select(group):
+        pick_t = sub_row == group * 8 + lax.shift_right_logical(lane_tile, 4)
+        chosen = jnp.where(pick_t, 1.0, 0.0).astype(BF16)
+        owner_lane = jnp.dot(owners, chosen, preferred_element_type=F32)[0:1]
+        return jnp.where(adapter_row == owner_lane, 1.0, 0.0)
+
+    selected = select(wa)
+    sel[0] = selected
+    sel[1] = select(far_half * NZ + z)
 
     def choose(full):
         kept = jnp.where(selected > 0.5, full, 0.0)
@@ -149,47 +162,47 @@
     lb[0, RANK : 2 * RANK] = choose(out_full)
 
     def l_copy(off):
-        return copy(lb.at[0], lb.at[off], l_s.at[off], l_r.at[off], dev_device(off))
+        return copy(lb.at[0], lb.at[off], l_s, l_r.at[off], dev_device(off))
 
     def w_copy(j):
         rows = pl.ds(pl.multiple_of(j * 2 * CH, 2 * CH), 2 * CH)
-        return copy(w_any.at[rows], w2.at[rows], w_s.at[j], w_r.at[j], far_dev)
+        return copy(w_any.at[rows], w2.at[rows], w_s, w_r.at[j], far_dev)
 
     def z_send(off):
         zt = lax.rem(z + off, NZ)
-        return copy(gs.at[zt], gf.at[z, sh], z_s.at[off], z_r.at[off], z_device(off))
+        return copy(gs.at[zt], gf.at[z, sh], z_s, z_r.at[off], z_device(off))
 
     def source(q):
         return lax.rem(z + OFFSETS[q], NZ)
 
     def x_send(q, step):
         band = gf.at[source(q), sh]
-        return copy(band, band, x_s.at[step, q], x_r.at[step, q], x_device(step))
+        return copy(band, band, x_s, x_r.at[step, q], x_device(step))
 
     def x_recv(q, step):
         band = gf.at[source(q), c * 4 + x_index(NX - step)]
-        return copy(band, band, x_s.at[step, q], x_r.at[step, q], x_device(step))
+        return copy(band, band, x_s, x_r.at[step, q], x_device(step))
 
     def core_send(q):
         block = gf.at[source(q), pl.ds(c * 4, 4)]
-        return copy(block, block, c_s.at[q], c_r.at[q], core_dev)
+        return copy(block, block, c_s, c_r.at[q], core_dev)
 
     def core_recv(q):
         block = gf.at[source(q), pl.ds((1 - c) * 4, 4)]
-        return copy(block, block, c_s.at[q], c_r.at[q], core_dev)
+        return copy(block, block, c_s, c_r.at[q], core_dev)
 
     pl.semaphore_wait(barrier, len(peers))
     for off in (1, 7, 2, 6, 3, 5, 4):
         z_send(off).start()
+    for off in range(1, NDEV):
+        l_copy(off).start()
     for j in range(EARLY_W):
         w_copy(j).start()
-    for off in range(1, NDEV):
-        l_copy(off).start()
     for q in range(NZ):
         if q > 0:
             off = NZ - OFFSETS[q]
             band = gf.at[source(q), sh]
-            copy(band, band, z_s.at[off], z_r.at[off], z_device(off)).wait_recv()
+            copy(band, band, z_s, z_r.at[off], z_device(off)).wait_recv()
         for step in (1, 3, 2):
             x_send(q, step).start()
 
@@ -198,37 +211,51 @@
     total = jnp.zeros((2 * RANK, ROWS), F32)
     for src in range(NDEV):
         total = total + lb[lax.rem(dev + NDEV - src, NDEV)]
-    summed = total.astype(BF16).astype(F32)
-    keep = sel[...] > 0.5
-
-    def spread(values):
+    lx[0] = total.astype(BF16)
+
+    def sums_copy():
+        return copy(lx.at[0], lx.at[1], k_s, k_r, far_dev)
+
+    def half_copy():
+        return copy(hs, hx.at[1], h_s, h_r, far_dev)
+
+    sums_copy().start()
+    half_copy().start()
+
+    def spread(which, first):
+        values = lx[which, first : first + RANK].astype(F32)
         wide = jnp.broadcast_to(values[None], (ADAPTERS, RANK, ROWS)).reshape(AR, ROWS)
-        return jnp.where(keep, wide, 0.0)
-
-    spread_in = spread(summed[0:RANK]).astype(BF16)
-    spread_out_wide = spread(summed[RANK : 2 * RANK])
-    spread_out = spread_out_wide.astype(BF16)
+        return jnp.where(sel[which] > 0.5, wide, 0.0)
+
+    spread_out_wide = spread(0, RANK)
+    so[0, :, :ROWS] = spread(0, 0).astype(BF16)
+    so[1, :, :ROWS] = spread_out_wide.astype(BF16)
     spread_out_t = spread_out_wide.T.astype(BF16)
 
     def adapter_step(k, carry):
         cols = pl.ds(pl.multiple_of(k * 256, 256), 256)
-        grad = 2.0 * jnp.dot(spread_out, hid[:, cols], preferred_element_type=F32)
-        pg[:, :, cols] = grad.reshape(ADAPTERS, RANK, 256)
         lo[:, cols] = 2.0 * jnp.dot(spread_out_t, a_ref[:, cols], preferred_element_type=F32)
         return carry
 
     lax.fori_loop(0, HID // 256, adapter_step, 0)
-    grad_b = 2.0 * jnp.dot(spread_in, gsl[...], preferred_element_type=F32)
-    pg[:, :, HID : HID + KG] = grad_b.reshape(ADAPTERS, RANK, KG)
-    for q in range(NZ):
-        sgf[q] = pg[(1 - yh) * NZ + q].astype(BF16)
-
-    def adapter_exchange():
-        return copy(sgf, grf, y_s, y_r, far_dev)
-
-    adapter_exchange().start()
-    for j in range(EARLY_W, NPAIR):
-        w_copy(j).start()
+
+    def adapter_grads():
+        sums_copy().wait_recv()
+        half_copy().wait_recv()
+        so[0, :, ROWS:] = spread(1, 0).astype(BF16)
+        so[1, :, ROWS:] = spread(1, RANK).astype(BF16)
+
+        def columns(which, cols, width):
+            left = jnp.concatenate([hx[0, :, cols], hx[1, :, cols]], axis=0)
+            grad = 2.0 * jnp.dot(so[which], left, preferred_element_type=F32)
+            pg[:, :, cols] = grad.reshape(ADAPTERS, RANK, width)
+
+        def grad_step(k, carry):
+            columns(1, pl.ds(pl.multiple_of(k * 128, 128), 128), 128)
+            return carry
+
+        lax.fori_loop(0, FH // 128, grad_step, 0)
+        columns(0, slice(FH, FH + GH), GH)
 
     for q in range(NZ):
         for step in (1, 3, 2):
@@ -245,7 +272,7 @@
         return lax.rem(z + NZ + (4 - s) * (1 - 2 * d), NZ)
 
     def b_copy(src, d, ch, s):
-        return copy(src, rbuf.at[d, ch, s], b_s.at[d, ch, s], b_r.at[d, ch, s], z_next(d))
+        return copy(src, rbuf.at[d, ch, s], b_s, b_r.at[d, ch, s], z_next(d))
 
     def a_copy(src, d, k, s):
         return copy(src, rg.at[d, k, s], a_s.at[d, k, s], a_r.at[d, k, s], z_next(d))
@@ -268,8 +295,10 @@
         hg_ref[:, cols] = base + lo[:, cols]
 
     def own_grads(k, zt):
-        cols = slice(k * GHALF, (k + 1) * GHALF)
-        return pg[yh * NZ + zt, :, cols] + grf[zt, :, cols].astype(F32)
+        return pg[k * NZ + zt]
+
+    def far_grads():
+        return copy(tb.at[far_half], gr, y_s, y_r, far_dev)
 
     def adapter_first(k, d, s):
         sg[k, s] = own_grads(k, target_z(d, s)).astype(BF16)
@@ -284,9 +313,9 @@
     def adapter_last(k):
         for d in range(2):
             a_copy(rg.at[d, k, 3], d, k, 3).wait_recv()
-        og_ref[:, k * GHALF : (k + 1) * GHALF] = (
-            own_grads(k, z) + rg[0, k, 3].astype(F32) + rg[1, k, 3].astype(F32)
-        )
+        done = own_grads(k, z) + rg[0, k, 3].astype(F32) + rg[1, k, 3].astype(F32)
+        tg[k] = done
+        tb[k] = done.astype(BF16)
 
     def product(j):
         rows = pl.ds(pl.multiple_of(j * 2 * CH, 2 * CH), 2 * CH)
@@ -308,6 +337,10 @@
     def tick(t, carry):
         @pl.when((t < NCH) & (lax.rem(t, 2) == 0))
         def _():
+            @pl.when(lax.div(t, 2) + EARLY_W < NPAIR)
+            def _():
+                w_copy(lax.div(t, 2) + EARLY_W).start()
+
             product(lax.div(t, 2))
 
         @pl.when(t < NCH)
@@ -326,9 +359,9 @@
                 else:
                     base_forward(ch, 1 - d4, s)
 
-        @pl.when(t == GTICK)
+        @pl.when(t == ATICK)
         def _():
-            adapter_exchange().wait_recv()
+            adapter_grads()
 
         for k in range(2):
             @pl.when(t == GTICK + k)
@@ -349,6 +382,10 @@
             def _(k=k):
                 adapter_last(k)
 
+        @pl.when(t == GTICK + 2 + 4 * LAG)
+        def _():
+            far_grads().start()
+
         ch = t - 4 * LAG
 
         @pl.when(ch >= 0)
@@ -359,37 +396,33 @@
 
     lax.fori_loop(0, NCH + 4 * LAG, tick, 0)
 
-    adapter_exchange().wait_send()
-    for off in range(1, NZ):
-        z_send(off).wait_send()
-    for off in range(1, NDEV):
-        l_copy(off).wait_send()
-    for q in range(NZ):
-        for step in (1, 2, 3):
-            x_send(q, step).wait_send()
-        core_send(q).wait_send()
-    for j in range(NPAIR):
-        w_copy(j).wait_send()
+    far_grads().wait_recv()
+    og_ref[pl.ds(yh, 1)] = tg[pl.ds(yh, 1)]
+    og_ref[pl.ds(far_half, 1)] = gr[...].astype(F32)[None]
+
+    def sent(block, sem):
+        copy(block, block, sem, k_r, far_dev).wait_send()
+
+    far_grads().wait_send()
+    sums_copy().wait_send()
+    half_copy().wait_send()
+    sent(gf.at[0, 0 : NZ - 1], z_s)
+    sent(lb.at[1:NDEV], l_s)
+    sent(gf.at[0 : NX - 1], x_s)
+    sent(gf.at[0 : NZ // 2], c_s)
+    sent(w2, w_s)
     for k in range(2):
         for d in range(2):
             for s in range(4):
                 if s > 0 or d == k % 2:
                     a_copy(rg.at[d, k, s], d, k, s).wait_send()
-
-    def drain_b(ch, carry):
-        d4 = lax.rem(ch, 2)
-        b_copy(rbuf.at[d4, ch, 0], d4, ch, 0).wait_send()
-        for d in range(2):
-            for s in range(1, 4):
-                b_copy(rbuf.at[d, ch, s], d, ch, s).wait_send()
-        return carry
-
-    lax.fori_loop(0, NCH, drain_b, 0)
+    sent(part.at[0 : NCH // 2, 0 : NZ - 1], b_s)
 
 
 def finish(hg_ref, og_ref, gate_ref, up_ref, ogate_ref, oup_ref, oga_ref, ogb_ref):
-    oga_ref[...] = og_ref[:, :HID]
-    ogb_ref[...] = og_ref[:, HID:]
+    for h in range(2):
+        oga_ref[:, h * FH : (h + 1) * FH] = og_ref[h, :, :FH]
+        ogb_ref[:, h * GH : (h + 1) * GH] = og_ref[h, :, FH:]
 
     def step(k, carry):
         cols = pl.ds(pl.multiple_of(k * 256, 256), 256)
@@ -413,7 +446,7 @@
         kernel,
         out_shape=(
             jax.ShapeDtypeStruct((ROWS, HID), F32),
-            jax.ShapeDtypeStruct((RANK, GCOL), F32),
+            jax.ShapeDtypeStruct((2, RANK, GHALF), F32),
         ),
         in_specs=[anywhere] * 6 + [whole] * 2,
         out_specs=(whole,) * 2,
@@ -431,23 +464,30 @@
             vmem((NCH, NZ, ROWS, CH), F32),
             vmem((2, NCH, 4, ROWS, CH), BF16),
             vmem((NCH, 2, ROWS, CH), BF16),
-            vmem((ADAPTERS, RANK, GCOL), F32),
+            vmem((ADAPTERS, RANK, GHALF), F32),
             vmem((2, 2, 4, RANK, GHALF), BF16),
             vmem((2, 2, RANK, GHALF), BF16),
-            vmem((NZ, RANK, GCOL), BF16),
-            vmem((NZ, RANK, GCOL), BF16),
+            vmem((ROWS, GHALF), BF16),
+            vmem((2, ROWS, GHALF), BF16),
+            vmem((2, AR, 2 * ROWS), BF16),
+            vmem((2, 2 * RANK, ROWS), BF16),
+            vmem((2, RANK, GHALF), F32),
+            vmem((2, RANK, GHALF), BF16),
+            vmem((RANK, GHALF), BF16),
             vmem((ROWS, KG), BF16),
             vmem((ROWS, HID), F32),
             vmem((NDEV, 2 * RANK, ROWS), F32),
-            vmem((AR, ROWS), F32),
+            vmem((2, AR, ROWS), F32),
             dma((7,)),
-            dma((NPAIR,)), dma((NPAIR,)),
-            dma((NZ,)), dma((NZ,)),
-            dma((NX, NZ)), dma((NX, NZ)),
-            dma((NZ,)), dma((NZ,)),
-            dma((NDEV,)), dma((NDEV,)),
-            dma((2, NCH, 4)), dma((2, NCH, 4)),
+            dma, dma((NPAIR,)),
+            dma, dma((NZ,)),
+            dma, dma((NX, NZ)),
+            dma, dma((NZ,)),
+            dma, dma((NDEV,)),
+            dma, dma((2, NCH, 4)),
             dma((2, 2, 4)), dma((2, 2, 4)),
+            dma, dma,
+            dma, dma,
             dma, dma,
         ],
         compiler_params=pltpu.CompilerParams(

time: 102 us -> 90.5 us (0.89)
  Pallas kernels: 101 us -> 89.4 us
    pallas_call x1, Pallas kernels: 98.1 us -> 86.4 us  [on_device(): pl.pallas_call(kernel, out_shape=(jax.ShapeDtypeStruct((ROWS, HID), F32),...]
where the time goes in v3:
time: 90.5 us; the launch traced here: 90 us
  Pallas kernels  89.4 us (99%)
    pallas_call x1, Pallas kernels, on_device(): pl.pallas_call(kernel, out_shape=(jax.ShapeDtypeStruct((ROWS, HID), F32),...  86.4 us
    pallas_call x1, Pallas kernels, on_device(): pl.pallas_call(finish, out_shape=(jax.ShapeDtypeStruct((ROWS, HID), BF16)...  2.99 us

profile of v3, /device:TPU:2, one launch (start us, length us, event | category | flops | bytes accessed | tf_op | source)
XLA Modules:
  0.0 90.0 jit_solution(3238737021412061225)
XLA Ops:
  0.6 86.4 %shard_map.111 = (f32[128,1792]{1,0:T(8,128)}, f32[2,16,1152]{2,1,0:T(8,128)}) custom-call(bf16[128,8192]{1,0:T(8,128)(2,1)} %g_any.1, bf16[1792,512]{1,0:T(8,128)(2,1)} %w_any.1, bf16[128,1792]{1,0:T(8,128)(2,1)} %gate_ref.1, bf16[128,1792]{1,0:T(8,128)(2,1)} %up_ref.1, bf16[256,1792]{1,0:T(8,128)(2,1)} %bitcast.6, bf16[256,512]{1,0:T(8,128)(2,1)} %bitcast.7, ...), custom_call_target="tpu_custom_call" | custom-call | tf_op jit(solution)/shard_map/pallas_call | solution.py:445
  87.0 3.0 %shard_map.112 = (bf16[128,1792]{1,0:T(8,128)(2,1)}, bf16[128,1792]{1,0:T(8,128)(2,1)}, f32[16,1792]{1,0:T(8,128)}, f32[16,512]{1,0:T(8,128)}) custom-call(f32[128,1792]{1,0:T(8,128)} %get-tuple-element.10.hg_ref, f32[2,16,1152]{2,1,0:T(8,128)} %get-tuple-element.11.og_ref, bf16[128,1792]{1,0:T(8,128)(2,1)} %gate_ref.1, bf16[128,1792]{1,0:T(8,128)(2,1)} %up_ref.1), custom_call_target="tpu_custom_call" | custom-call | tf_op jit(solution)/shard_map/pallas_call | solution.py:501

commit v4 on v3

--- a/solution.py
+++ b/solution.py
@@ -14,12 +14,11 @@
 CH = 128
 NCH = HID // CH
 NPAIR = NCH // 2
-LAG = 2
 GCOL = HID + 512
 GHALF = GCOL // 2
-GTICK = 8
-ATICK = 5
-EARLY_W = 2
+GITEM = 2
+ITEMS = NPAIR + 1
+EARLY_W = 3
 FH = HID // 2
 GH = KG // 2
 RANK = 16
@@ -40,8 +39,8 @@
     g_any, w_any, gate_any, up_any, a_any, b_any, owner_ref, live_ref,
     hg_ref, og_ref,
     w_ref, a_ref, b_ref, gate_ref, up_ref, gsh,
-    gs, gf, w2, hid, part, rbuf, sbuf, pg, rg, sg, hs, hx, so, lx, tg, tb, gr, gsl, lo, lb, sel,
-    ld, w_s, w_r, z_s, z_r, x_s, x_r, c_s, c_r, l_s, l_r,
+    gs, gf, w2, hid, part, rbuf, sbuf, pg, rg, sg, hs, hx, so, lx, tg, tb, gr, gsl, lo, lb, ls, sel,
+    ld, w_s, w_r, z_s, z_r, x_s, x_r, c_s, c_r, l_s, l_r, t_s, t_r,
     b_s, b_r, a_s, a_r, h_s, h_r, k_s, k_r, y_s, y_r,
 ):
     wa = lax.axis_index("wa")
@@ -64,8 +63,10 @@
 
     core_dev = (wa, yl * 8 + x * 2 + (1 - c))
 
-    def dev_device(off):
-        return (wa, lax.rem(dev + off, NDEV))
+    def low_device(off):
+        return (wa, yl * 8 + lax.rem(low + off, 8))
+
+    side_dev = (wa, lax.rem(dev + 8, NDEV))
 
     def copy(src, dst, ssem, rsem, target):
         return pltpu.make_async_remote_copy(
@@ -74,8 +75,8 @@
         )
 
     barrier = pltpu.get_barrier_semaphore()
-    peers = [z_device(o) for o in (4, 3, 5, 2, 6, 1, 7)] + [far_dev]
-    peers += [dev_device(o) for o in range(1, NDEV)]
+    peers = [z_device(o) for o in (4, 3, 5, 2, 6, 1, 7)] + [far_dev, side_dev]
+    peers += [low_device(o) for o in range(1, 8)]
     for peer in peers:
         pl.semaphore_signal(barrier, inc=1, device_id=peer, device_id_type=MESH)
 
@@ -162,7 +163,7 @@
     lb[0, RANK : 2 * RANK] = choose(out_full)
 
     def l_copy(off):
-        return copy(lb.at[0], lb.at[off], l_s, l_r.at[off], dev_device(off))
+        return copy(lb.at[0], lb.at[off], l_s, l_r.at[off], low_device(off))
 
     def w_copy(j):
         rows = pl.ds(pl.multiple_of(j * 2 * CH, 2 * CH), 2 * CH)
@@ -194,10 +195,13 @@
     pl.semaphore_wait(barrier, len(peers))
     for off in (1, 7, 2, 6, 3, 5, 4):
         z_send(off).start()
-    for off in range(1, NDEV):
+    for off in range(1, 8):
         l_copy(off).start()
-    for j in range(EARLY_W):
-        w_copy(j).start()
+    w_copy(0).start()
+
+    def side_copy():
+        return copy(ls.at[0], ls.at[1], t_s, t_r, side_dev)
+
     for q in range(NZ):
         if q > 0:
             off = NZ - OFFSETS[q]
@@ -205,12 +209,18 @@
             copy(band, band, z_s, z_r.at[off], z_device(off)).wait_recv()
         for step in (1, 3, 2):
             x_send(q, step).start()
-
-    for off in range(1, NDEV):
-        l_copy(off).wait_recv()
-    total = jnp.zeros((2 * RANK, ROWS), F32)
-    for src in range(NDEV):
-        total = total + lb[lax.rem(dev + NDEV - src, NDEV)]
+        if q == 2:
+            for off in range(1, 8):
+                l_copy(off).wait_recv()
+            part_sum = jnp.zeros((2 * RANK, ROWS), F32)
+            for src in range(8):
+                part_sum = part_sum + lb[lax.rem(low + 8 - src, 8)]
+            ls[0] = part_sum
+            side_copy().start()
+            w_copy(1).start()
+
+    side_copy().wait_recv()
+    total = ls[0] + ls[1]
     lx[0] = total.astype(BF16)
 
     def sums_copy():
@@ -221,6 +231,8 @@
 
     sums_copy().start()
     half_copy().start()
+    for j in range(2, EARLY_W):
+        w_copy(j).start()
 
     def spread(which, first):
         values = lx[which, first : first + RANK].astype(F32)
@@ -334,67 +346,78 @@
 
         lax.fori_loop(0, NZ // 2, block, 0)
 
-    def tick(t, carry):
-        @pl.when((t < NCH) & (lax.rem(t, 2) == 0))
-        def _():
-            @pl.when(lax.div(t, 2) + EARLY_W < NPAIR)
-            def _():
-                w_copy(lax.div(t, 2) + EARLY_W).start()
-
-            product(lax.div(t, 2))
-
-        @pl.when(t < NCH)
-        def _():
-            base_first(t, lax.rem(t, 2), 0)
-
-        for s in (1, 2, 3):
-            ch = t - s * LAG
-
-            @pl.when((ch >= 0) & (ch < NCH))
-            def _(ch=ch, s=s):
-                d4 = lax.rem(ch, 2)
-                base_forward(ch, d4, s)
+    def base_step(p, s):
+        for h in range(2):
+            ch = 2 * p + h
+            if s == 0:
+                base_first(ch, h, 0)
+            else:
+                base_forward(ch, h, s)
                 if s == 1:
-                    base_first(ch, 1 - d4, s)
+                    base_first(ch, 1 - h, s)
                 else:
-                    base_forward(ch, 1 - d4, s)
-
-        @pl.when(t == ATICK)
+                    base_forward(ch, 1 - h, s)
+
+    def adapter_part(s):
+        for k in range(2):
+            if s == 0:
+                adapter_first(k, k, 0)
+            else:
+                adapter_forward(k, k, s)
+                if s == 1:
+                    adapter_first(k, 1 - k, s)
+                else:
+                    adapter_forward(k, 1 - k, s)
+
+    def pair_of(i):
+        return jnp.where(i > GITEM, i - 1, i)
+
+    def is_pair(i):
+        return (i >= 0) & (i < ITEMS) & (i != GITEM)
+
+    def item_step(i, s):
+        @pl.when(is_pair(i))
+        def _():
+            base_step(pair_of(i), s)
+
+        @pl.when(i == GITEM)
+        def _():
+            adapter_part(s)
+
+    def item(i, carry):
+        @pl.when(is_pair(i) & (pair_of(i) + EARLY_W < NPAIR))
+        def _():
+            w_copy(pair_of(i) + EARLY_W).start()
+
+        for s in (3, 2, 1):
+            item_step(i - s, s)
+
+        @pl.when(is_pair(i))
+        def _():
+            p = pair_of(i)
+
+            product(p)
+
+        @pl.when(i == GITEM)
         def _():
             adapter_grads()
 
-        for k in range(2):
-            @pl.when(t == GTICK + k)
-            def _(k=k):
-                adapter_first(k, k % 2, 0)
-
-            for s in (1, 2, 3):
-                @pl.when(t == GTICK + k + s * LAG)
-                def _(k=k, s=s):
-                    d4 = k % 2
-                    adapter_forward(k, d4, s)
-                    if s == 1:
-                        adapter_first(k, 1 - d4, s)
-                    else:
-                        adapter_forward(k, 1 - d4, s)
-
-            @pl.when(t == GTICK + k + 4 * LAG)
-            def _(k=k):
+        item_step(i, 0)
+
+        @pl.when(is_pair(i - 4))
+        def _():
+            for h in range(2):
+                base_last(2 * pair_of(i - 4) + h)
+
+        @pl.when(i - 4 == GITEM)
+        def _():
+            for k in range(2):
                 adapter_last(k)
-
-        @pl.when(t == GTICK + 2 + 4 * LAG)
-        def _():
             far_grads().start()
 
-        ch = t - 4 * LAG
-
-        @pl.when(ch >= 0)
-        def _():
-            base_last(ch)
-
         return carry
 
-    lax.fori_loop(0, NCH + 4 * LAG, tick, 0)
+    lax.fori_loop(0, ITEMS + 4, item, 0)
 
     far_grads().wait_recv()
     og_ref[pl.ds(yh, 1)] = tg[pl.ds(yh, 1)]
@@ -407,7 +430,8 @@
     sums_copy().wait_send()
     half_copy().wait_send()
     sent(gf.at[0, 0 : NZ - 1], z_s)
-    sent(lb.at[1:NDEV], l_s)
+    sent(lb.at[1:8], l_s)
+    side_copy().wait_send()
     sent(gf.at[0 : NX - 1], x_s)
     sent(gf.at[0 : NZ // 2], c_s)
     sent(w2, w_s)
@@ -476,14 +500,16 @@
             vmem((RANK, GHALF), BF16),
             vmem((ROWS, KG), BF16),
             vmem((ROWS, HID), F32),
-            vmem((NDEV, 2 * RANK, ROWS), F32),
+            vmem((8, 2 * RANK, ROWS), F32),
+            vmem((2, 2 * RANK, ROWS), F32),
             vmem((2, AR, ROWS), F32),
             dma((7,)),
             dma, dma((NPAIR,)),
             dma, dma((NZ,)),
             dma, dma((NX, NZ)),
             dma, dma((NZ,)),
-            dma, dma((NDEV,)),
+            dma, dma((8,)),
+            dma, dma,
             dma, dma((2, NCH, 4)),
             dma((2, 2, 4)), dma((2, 2, 4)),
             dma, dma,

time: 90.5 us -> 84.9 us (0.938)
  Pallas kernels: 89.4 us -> 83.1 us
    pallas_call x1, Pallas kernels: 86.4 us -> 80.1 us  [on_device(): pl.pallas_call(kernel, out_shape=(jax.ShapeDtypeStruct((ROWS, HID), F32),...]
where the time goes in v4:
time: 84.9 us; the launch traced here: 83.7 us
  Pallas kernels  83.1 us (98%)
    pallas_call x1, Pallas kernels, on_device(): pl.pallas_call(kernel, out_shape=(jax.ShapeDtypeStruct((ROWS, HID), F32),...  80.1 us
    pallas_call x1, Pallas kernels, on_device(): pl.pallas_call(finish, out_shape=(jax.ShapeDtypeStruct((ROWS, HID), BF16)...  2.99 us

profile of v4, /device:TPU:2, one launch (start us, length us, event | category | flops | bytes accessed | tf_op | source)
XLA Modules:
  0.0 83.7 jit_solution(10152969932771705177)
XLA Ops:
  0.6 80.1 %shard_map.111 = (f32[128,1792]{1,0:T(8,128)}, f32[2,16,1152]{2,1,0:T(8,128)}) custom-call(bf16[128,8192]{1,0:T(8,128)(2,1)} %g_any.1, bf16[1792,512]{1,0:T(8,128)(2,1)} %w_any.1, bf16[128,1792]{1,0:T(8,128)(2,1)} %gate_ref.1, bf16[128,1792]{1,0:T(8,128)(2,1)} %up_ref.1, bf16[256,1792]{1,0:T(8,128)(2,1)} %bitcast.6, bf16[256,512]{1,0:T(8,128)(2,1)} %bitcast.7, ...), custom_call_target="tpu_custom_call" | custom-call | tf_op jit(solution)/shard_map/pallas_call | solution.py:469
  80.7 3.0 %shard_map.112 = (bf16[128,1792]{1,0:T(8,128)(2,1)}, bf16[128,1792]{1,0:T(8,128)(2,1)}, f32[16,1792]{1,0:T(8,128)}, f32[16,512]{1,0:T(8,128)}) custom-call(f32[128,1792]{1,0:T(8,128)} %get-tuple-element.10.hg_ref, f32[2,16,1152]{2,1,0:T(8,128)} %get-tuple-element.11.og_ref, bf16[128,1792]{1,0:T(8,128)(2,1)} %gate_ref.1, bf16[128,1792]{1,0:T(8,128)(2,1)} %up_ref.1), custom_call_target="tpu_custom_call" | custom-call | tf_op jit(solution)/shard_map/pallas_call | solution.py:527

commit v5 on v4

--- a/solution.py
+++ b/solution.py
@@ -16,8 +16,6 @@
 NPAIR = NCH // 2
 GCOL = HID + 512
 GHALF = GCOL // 2
-GITEM = 2
-ITEMS = NPAIR + 1
 EARLY_W = 3
 FH = HID // 2
 GH = KG // 2
@@ -197,7 +195,11 @@
         z_send(off).start()
     for off in range(1, 8):
         l_copy(off).start()
-    w_copy(0).start()
+
+    def half_copy():
+        return copy(hs, hx.at[1], h_s, h_r, far_dev)
+
+    half_copy().start()
 
     def side_copy():
         return copy(ls.at[0], ls.at[1], t_s, t_r, side_dev)
@@ -217,7 +219,6 @@
                 part_sum = part_sum + lb[lax.rem(low + 8 - src, 8)]
             ls[0] = part_sum
             side_copy().start()
-            w_copy(1).start()
 
     side_copy().wait_recv()
     total = ls[0] + ls[1]
@@ -226,12 +227,8 @@
     def sums_copy():
         return copy(lx.at[0], lx.at[1], k_s, k_r, far_dev)
 
-    def half_copy():
-        return copy(hs, hx.at[1], h_s, h_r, far_dev)
-
     sums_copy().start()
-    half_copy().start()
-    for j in range(2, EARLY_W):
+    for j in range(EARLY_W):
         w_copy(j).start()
 
     def spread(which, first):
@@ -268,14 +265,6 @@
 
         lax.fori_loop(0, FH // 128, grad_step, 0)
         columns(0, slice(FH, FH + GH), GH)
-
-    for q in range(NZ):
-        for step in (1, 3, 2):
-            x_recv(q, step).wait_recv()
-        core_send(q).start()
-    for q in range(NZ):
-        core_recv(q).wait_recv()
-    loads[6].wait()
 
     def z_next(d):
         return (yh * NZ + lax.rem(z + 1 + 6 * d, NZ), dev)
@@ -369,55 +358,54 @@
                 else:
                     adapter_forward(k, 1 - k, s)
 
-    def pair_of(i):
-        return jnp.where(i > GITEM, i - 1, i)
-
-    def is_pair(i):
-        return (i >= 0) & (i < ITEMS) & (i != GITEM)
-
-    def item_step(i, s):
-        @pl.when(is_pair(i))
+    for q in range(NZ):
+        for step in (1, 3, 2):
+            x_recv(q, step).wait_recv()
+        core_send(q).start()
+    adapter_grads()
+    adapter_part(0)
+    for q in range(NZ):
+        core_recv(q).wait_recv()
+    loads[6].wait()
+
+    def item_step(p, s):
+        @pl.when((p >= 0) & (p < NPAIR))
         def _():
-            base_step(pair_of(i), s)
-
-        @pl.when(i == GITEM)
+            base_step(p, s)
+
+    def item(i, carry):
+        @pl.when(i + EARLY_W < NPAIR)
         def _():
-            adapter_part(s)
-
-    def item(i, carry):
-        @pl.when(is_pair(i) & (pair_of(i) + EARLY_W < NPAIR))
-        def _():
-            w_copy(pair_of(i) + EARLY_W).start()
+            w_copy(i + EARLY_W).start()
 
         for s in (3, 2, 1):
             item_step(i - s, s)
 
-        @pl.when(is_pair(i))
+        @pl.when(i < NPAIR)
         def _():
-            p = pair_of(i)
-
-            product(p)
-
-        @pl.when(i == GITEM)
-        def _():
-            adapter_grads()
+            product(i)
 
         item_step(i, 0)
 
-        @pl.when(is_pair(i - 4))
-        def _():
-            for h in range(2):
-                base_last(2 * pair_of(i - 4) + h)
-
-        @pl.when(i - 4 == GITEM)
+        for s in (1, 2, 3):
+            @pl.when(i == s - 1)
+            def _(s=s):
+                adapter_part(s)
+
+        @pl.when(i == 3)
         def _():
             for k in range(2):
                 adapter_last(k)
             far_grads().start()
 
+        @pl.when(i >= 4)
+        def _():
+            for h in range(2):
+                base_last(2 * (i - 4) + h)
+
         return carry
 
-    lax.fori_loop(0, ITEMS + 4, item, 0)
+    lax.fori_loop(0, NPAIR + 4, item, 0)
 
     far_grads().wait_recv()
     og_ref[pl.ds(yh, 1)] = tg[pl.ds(yh, 1)]
@@ -444,12 +432,11 @@
 
 
 def finish(hg_ref, og_ref, gate_ref, up_ref, ogate_ref, oup_ref, oga_ref, ogb_ref):
-    for h in range(2):
-        oga_ref[:, h * FH : (h + 1) * FH] = og_ref[h, :, :FH]
-        ogb_ref[:, h * GH : (h + 1) * GH] = og_ref[h, :, FH:]
+    oga_ref[...] = og_ref[0, :, :FH]
+    ogb_ref[...] = og_ref[0, :, FH:]
 
     def step(k, carry):
-        cols = pl.ds(pl.multiple_of(k * 256, 256), 256)
+        cols = pl.ds(pl.multiple_of(k * CH, CH), CH)
         grad = hg_ref[:, cols]
         gate = gate_ref[:, cols].astype(F32)
         up_value = up_ref[:, cols].astype(F32)
@@ -458,7 +445,7 @@
         ogate_ref[:, cols] = (grad * up_value * s * (1.0 + gate * (1.0 - s))).astype(BF16)
         return carry
 
-    lax.fori_loop(0, HID // 256, step, 0)
+    lax.fori_loop(0, FH // CH, step, 0)
 
 
 def on_device(grad, weight, gate, up, down_factor, up_factor, owner, live):
@@ -524,6 +511,7 @@
         down_factor.reshape(AR, HID), up_factor.reshape(AR, KG),
         owner.reshape(1, owner.shape[0]), live.reshape(1, live.shape[0]),
     )
+    wide = pl.BlockSpec((ROWS, FH), lambda h: (0, h))
     out_gate, out_up, grad_a, grad_b = pl.pallas_call(
         finish,
         out_shape=(
@@ -532,8 +520,14 @@
             jax.ShapeDtypeStruct((RANK, HID), F32),
             jax.ShapeDtypeStruct((RANK, KG), F32),
         ),
-        in_specs=[whole] * 4,
-        out_specs=(whole,) * 4,
+        grid=(2,),
+        in_specs=[wide, pl.BlockSpec((1, RANK, GHALF), lambda h: (h, 0, 0)), wide, wide],
+        out_specs=(
+            wide,
+            wide,
+            pl.BlockSpec((RANK, FH), lambda h: (0, h)),
+            pl.BlockSpec((RANK, GH), lambda h: (0, h)),
+        ),
     )(hidden_grad, adapter_grads, gate, up)
     return out_gate, out_up, grad_a[None], grad_b[None]
 

time: 84.9 us -> 83.6 us (0.985); the launches traced: 83.7 us -> 83.4 us
  no operation moved by 1% of the time
where the time goes in v5:
time: 83.6 us; the launch traced here: 83.4 us
  Pallas kernels  82.8 us (99%)
    pallas_call x1, Pallas kernels, on_device(): pl.pallas_call(kernel, out_shape=(jax.ShapeDtypeStruct((ROWS, HID), F32),...  80.1 us
    pallas_call x1, Pallas kernels, on_device(): pl.pallas_call(finish, out_shape=(jax.ShapeDtypeStruct((ROWS, HID), BF16)...  2.64 us

profile of v5, /device:TPU:2, one launch (start us, length us, event | category | flops | bytes accessed | tf_op | source)
XLA Modules:
  0.0 83.4 jit_solution(14583221526755673409)
XLA Ops:
  0.6 80.1 %shard_map.111 = (f32[128,1792]{1,0:T(8,128)}, f32[2,16,1152]{2,1,0:T(8,128)}) custom-call(bf16[128,8192]{1,0:T(8,128)(2,1)} %g_any.1, bf16[1792,512]{1,0:T(8,128)(2,1)} %w_any.1, bf16[128,1792]{1,0:T(8,128)(2,1)} %gate_ref.1, bf16[128,1792]{1,0:T(8,128)(2,1)} %up_ref.1, bf16[256,1792]{1,0:T(8,128)(2,1)} %bitcast.6, bf16[256,512]{1,0:T(8,128)(2,1)} %bitcast.7, ...), custom_call_target="tpu_custom_call" | custom-call | tf_op jit(solution)/shard_map/pallas_call | solution.py:456
  80.8 2.6 %shard_map.112 = (bf16[128,1792]{1,0:T(8,128)(2,1)}, bf16[128,1792]{1,0:T(8,128)(2,1)}, f32[16,1792]{1,0:T(8,128)}, f32[16,512]{1,0:T(8,128)}) custom-call(f32[128,1792]{1,0:T(8,128)} %get-tuple-element.10.hg_ref, f32[2,16,1152]{2,1,0:T(8,128)} %get-tuple-element.11.og_ref, bf16[128,1792]{1,0:T(8,128)(2,1)} %gate_ref.1, bf16[128,1792]{1,0:T(8,128)(2,1)} %up_ref.1), custom_call_target="tpu_custom_call" | custom-call | tf_op jit(solution)/shard_map/pallas_call | solution.py:515

commit v6 on v5

--- a/solution.py
+++ b/solution.py
@@ -16,7 +16,7 @@
 NPAIR = NCH // 2
 GCOL = HID + 512
 GHALF = GCOL // 2
-EARLY_W = 3
+EARLY_W = 4
 FH = HID // 2
 GH = KG // 2
 RANK = 16
@@ -209,7 +209,7 @@
             off = NZ - OFFSETS[q]
             band = gf.at[source(q), sh]
             copy(band, band, z_s, z_r.at[off], z_device(off)).wait_recv()
-        for step in (1, 3, 2):
+        for step in (2, 1, 3):
             x_send(q, step).start()
         if q == 2:
             for off in range(1, 8):
@@ -359,7 +359,7 @@
                     adapter_forward(k, 1 - k, s)
 
     for q in range(NZ):
-        for step in (1, 3, 2):
+        for step in (2, 1, 3):
             x_recv(q, step).wait_recv()
         core_send(q).start()
     adapter_grads()

time: 83.6 us -> 83.5 us (level)
  no operation moved by 1% of the time
where the time goes in v6:
time: 83.5 us; the launch traced here: 83.4 us
  Pallas kernels  82.8 us (99%)
    pallas_call x1, Pallas kernels, on_device(): pl.pallas_call(kernel, out_shape=(jax.ShapeDtypeStruct((ROWS, HID), F32),...  80.1 us
    pallas_call x1, Pallas kernels, on_device(): pl.pallas_call(finish, out_shape=(jax.ShapeDtypeStruct((ROWS, HID), BF16)...  2.64 us

profile of v6, /device:TPU:2, one launch (start us, length us, event | category | flops | bytes accessed | tf_op | source)
XLA Modules:
  0.0 83.4 jit_solution(17358404570244419523)
XLA Ops:
  0.6 80.1 %shard_map.111 = (f32[128,1792]{1,0:T(8,128)}, f32[2,16,1152]{2,1,0:T(8,128)}) custom-call(bf16[128,8192]{1,0:T(8,128)(2,1)} %g_any.1, bf16[1792,512]{1,0:T(8,128)(2,1)} %w_any.1, bf16[128,1792]{1,0:T(8,128)(2,1)} %gate_ref.1, bf16[128,1792]{1,0:T(8,128)(2,1)} %up_ref.1, bf16[256,1792]{1,0:T(8,128)(2,1)} %bitcast.6, bf16[256,512]{1,0:T(8,128)(2,1)} %bitcast.7, ...), custom_call_target="tpu_custom_call" | custom-call | tf_op jit(solution)/shard_map/pallas_call | solution.py:456
  80.8 2.6 %shard_map.112 = (bf16[128,1792]{1,0:T(8,128)(2,1)}, bf16[128,1792]{1,0:T(8,128)(2,1)}, f32[16,1792]{1,0:T(8,128)}, f32[16,512]{1,0:T(8,128)}) custom-call(f32[128,1792]{1,0:T(8,128)} %get-tuple-element.10.hg_ref, f32[2,16,1152]{2,1,0:T(8,128)} %get-tuple-element.11.og_ref, bf16[128,1792]{1,0:T(8,128)(2,1)} %gate_ref.1, bf16[128,1792]{1,0:T(8,128)(2,1)} %up_ref.1), custom_call_target="tpu_custom_call" | custom-call | tf_op jit(solution)/shard_map/pallas_call | solution.py:515
